TPU v7x, 128 devices: a whole 4x4x4 slice. The times are simulated.
128 devices in a mesh: seq: 32 (over z, y, x_hi), ch: 4 (over x_lo, core).
Axes of the slice: x: 4 (x_hi: 2, x_lo: 2; x = x_hi * 2 + x_lo), y: 4, z: 4, core: 2. Of those that a mesh axis runs over, the one named last changes fastest.
Arguments:
- attn_query: bfloat16 [4096, 4096], P(('seq', 'ch')), may hold values from -6 to 6
- attn_key: bfloat16 [4096, 4096], P(('seq', 'ch')), may hold values from -6 to 6
- attn_value: bfloat16 [4096, 4096], P(('seq', 'ch')), may hold values from -6 to 6
- attn_output: bfloat16 [4096, 4096], P(('seq', 'ch')), may hold values from -1.796875 to 1.796875
- attn_grad_out: bfloat16 [4096, 4096], P(('seq', 'ch')), may hold values from -6 to 6
- conv_query: bfloat16 [4096, 8192], P(('seq', 'ch')), may hold values from -6 to 6
- conv_key: bfloat16 [4096, 8192], P(('seq', 'ch')), may hold values from -6 to 6
- conv_value: bfloat16 [4096, 8192], P(('seq', 'ch')), may hold values from -6 to 6
- conv_grad_out: bfloat16 [4096, 8192], P(('seq', 'ch')), may hold values from -6 to 6
- conv_filter: bfloat16 [512, 128], P('ch'), may hold values from -0.5 to 0.5
- doc_lengths: int32 [12], replicated, may hold values from 1 to 1280, 4096 in all
Outputs:
- grad_attn_query: bfloat16 [4096, 4096], P(('seq', 'ch'))
- grad_attn_key: bfloat16 [4096, 4096], P(('seq', 'ch'))
- grad_attn_value: bfloat16 [4096, 4096], P(('seq', 'ch'))
- grad_conv_query: bfloat16 [4096, 8192], P(('seq', 'ch'))
- grad_conv_key: bfloat16 [4096, 8192], P(('seq', 'ch'))
- grad_conv_value: bfloat16 [4096, 8192], P(('seq', 'ch'))
- grad_filter: float32 [512, 128], P('ch')
Inputs may be any that keep to these rules, and one draw needn't show every extreme that they name: `doc_lengths`: the lengths of 12 documents laid end to end in the window; they sum to 4096 and the longest has exactly 1280 positions.
All inputs are finite; a program needn't handle non-finite values.
Results may differ from a plain program's by a relative error of at most 0.0049.
Values may be sent and summed in bfloat16 or wider, within the bound.
A program may use at most 128 MiB of HBM per device.

v0:
```python
import math

import jax
import jax.numpy as jnp
from jax import lax
from jax.sharding import PartitionSpec as P

HEAD_DIM = 128
GROUP = 16
FILTER_LEN = 128


NEG_FILL = -1e30


def passed_along(block, axis, distance):
    devices = range(lax.axis_size(axis))
    route = [(i - distance, i) for i in devices if i - distance in devices]
    return lax.ppermute(block, axis, route)


def doc_index(doc_lengths, positions):
    doc_ends = jnp.cumsum(doc_lengths)
    return jnp.sum((doc_ends[None, :] <= positions[:, None]).astype(jnp.int32), axis=1)


def banded(taps, row_count):
    group_count, tap_count = taps.shape
    span_count = row_count + tap_count - 1
    padded = jnp.pad(taps, ((0, 0), (0, row_count)))
    repeated = jnp.tile(padded, (1, row_count))[:, : row_count * span_count]
    return repeated.reshape(group_count, row_count, span_count)


def band_sums(matrix, tap_count):
    group_count, row_count, span_count = matrix.shape
    padded = jnp.pad(matrix, ((0, 0), (0, 0), (0, 1)))
    flattened = jnp.pad(
        padded.reshape(group_count, row_count * (span_count + 1)), ((0, 0), (0, row_count))
    )
    skewed = flattened.reshape(group_count, row_count, span_count + 2)
    return jnp.sum(skewed[:, :, :tap_count], axis=1)


def body(
    attn_query,
    attn_key,
    attn_value,
    attn_output,
    attn_grad_out,
    conv_query,
    conv_key,
    conv_value,
    conv_grad_out,
    conv_filter,
    doc_lengths,
):
    (
        query_rows,
        key_rows,
        value_rows,
        output_rows,
        grad_rows,
        mixer_query,
        mixer_key,
        mixer_value,
        mixer_grad,
    ) = (
        lax.all_to_all(attn_query, "ch", split_axis=1, concat_axis=0, tiled=True),
        lax.all_to_all(attn_key, "ch", split_axis=1, concat_axis=0, tiled=True),
        lax.all_to_all(attn_value, "ch", split_axis=1, concat_axis=0, tiled=True),
        lax.all_to_all(attn_output, "ch", split_axis=1, concat_axis=0, tiled=True),
        lax.all_to_all(attn_grad_out, "ch", split_axis=1, concat_axis=0, tiled=True),
        lax.all_to_all(conv_query, "ch", split_axis=1, concat_axis=0, tiled=True),
        lax.all_to_all(conv_key, "ch", split_axis=1, concat_axis=0, tiled=True),
        lax.all_to_all(conv_value, "ch", split_axis=1, concat_axis=0, tiled=True),
        lax.all_to_all(conv_grad_out, "ch", split_axis=1, concat_axis=0, tiled=True),
    )
    seq_count = lax.axis_size("seq")
    tok_rows = query_rows.shape[0]
    total_tokens = tok_rows * seq_count
    most_tokens = total_tokens * 5 // 16
    span_steps = (most_tokens - 2) // tok_rows + 1
    head_count = query_rows.shape[1] // HEAD_DIM
    scale_factor = 1.0 / math.sqrt(HEAD_DIM)
    row_base = lax.axis_index("seq") * tok_rows
    local_pos = row_base + jnp.arange(tok_rows, dtype=jnp.int32)
    local_doc = doc_index(doc_lengths, local_pos)
    query_heads = query_rows.reshape(tok_rows, head_count, HEAD_DIM)
    key_heads = key_rows.reshape(tok_rows, head_count, HEAD_DIM)
    value_heads = value_rows.reshape(tok_rows, head_count, HEAD_DIM)
    output_heads = output_rows.reshape(tok_rows, head_count, HEAD_DIM)
    grad_heads = grad_rows.reshape(tok_rows, head_count, HEAD_DIM)
    delta_rows = jnp.sum(grad_heads.astype(jnp.float32) * output_heads.astype(jnp.float32), axis=2)
    delta_heads = delta_rows.T

    def key_step(carried, pieces, key_start):
        key_part, value_part = pieces
        key_pos = key_start + jnp.arange(key_part.shape[0], dtype=jnp.int32)
        key_doc = doc_index(doc_lengths, key_pos)
        visible = (
            (key_doc[None, :] == local_doc[:, None])
            & (key_pos[None, :] <= local_pos[:, None])
            & (key_pos[None, :] >= 0)
        )
        running_max, running_sum, running_grad = carried
        scores = (
            jnp.einsum("thd,rhd->htr", query_heads, key_part, preferred_element_type=jnp.float32)
            * scale_factor
        )
        new_max = jnp.maximum(
            running_max, jnp.max(jnp.where(visible[None], scores, NEG_FILL), axis=2)
        )
        weights = jnp.where(visible[None], jnp.exp(scores - new_max[:, :, None]), 0.0)
        rescale = jnp.exp(running_max - new_max)
        grad_probs = jnp.einsum(
            "thd,rhd->htr", grad_heads, value_part, preferred_element_type=jnp.float32
        )
        weighted = weights * (grad_probs - delta_heads[:, :, None])
        update = jnp.einsum(
            "htr,rhd->htd", weighted, key_part.astype(jnp.float32), precision=lax.Precision.HIGHEST
        )
        return (
            new_max,
            running_sum * rescale + jnp.sum(weights, axis=2),
            running_grad * rescale[:, :, None] + update,
        )

    start_state = (
        jnp.full((head_count, tok_rows), NEG_FILL, jnp.float32),
        jnp.zeros((head_count, tok_rows), jnp.float32),
        jnp.zeros((head_count, tok_rows, HEAD_DIM), jnp.float32),
    )
    first_state = key_step(start_state, (key_heads, value_heads), row_base)

    def key_chain(step_index, loop_state):
        carried, travelling = loop_state
        travelling = passed_along(travelling, "seq", 1)
        carried = key_step(
            carried, (travelling[0], travelling[1]), row_base - (step_index + 1) * tok_rows
        )
        return (carried, travelling)

    chain_state = lax.fori_loop(
        0, span_steps, key_chain, (first_state, jnp.stack((key_heads, value_heads)))
    )
    final_max, final_sum, final_grad = chain_state[0]
    lse_heads = final_max + jnp.log(final_sum)
    lse_rows = lse_heads.T
    grad_query = (final_grad * (scale_factor / final_sum)[:, :, None]).transpose(1, 0, 2)
    grad_query = grad_query.reshape(tok_rows, head_count * HEAD_DIM).astype(jnp.bfloat16)

    def query_step(carried, pieces, query_start, lse_part, delta_part):
        query_part, grad_part = pieces
        query_pos = query_start + jnp.arange(query_part.shape[0], dtype=jnp.int32)
        query_doc = doc_index(doc_lengths, query_pos)
        visible = (
            (query_doc[:, None] == local_doc[None, :])
            & (local_pos[None, :] <= query_pos[:, None])
            & (query_pos[:, None] < total_tokens)
        )
        key_grad, value_grad = carried
        scores = (
            jnp.einsum("rhd,thd->hrt", query_part, key_heads, preferred_element_type=jnp.float32)
            * scale_factor
        )
        probs = jnp.where(visible[None], jnp.exp(scores - lse_part.T[:, :, None]), 0.0)
        value_grad = value_grad + jnp.einsum(
            "hrt,rhd->thd", probs, grad_part.astype(jnp.float32), precision=lax.Precision.HIGHEST
        )
        grad_probs = jnp.einsum(
            "rhd,thd->hrt", grad_part, value_heads, preferred_element_type=jnp.float32
        )
        grad_scores = probs * (grad_probs - delta_part.T[:, :, None])
        key_grad = key_grad + scale_factor * jnp.einsum(
            "hrt,rhd->thd",
            grad_scores,
            query_part.astype(jnp.float32),
            precision=lax.Precision.HIGHEST,
        )
        return (key_grad, value_grad)

    zero_grads = (
        jnp.zeros((tok_rows, head_count, HEAD_DIM), jnp.float32),
        jnp.zeros((tok_rows, head_count, HEAD_DIM), jnp.float32),
    )
    first_grads = query_step(zero_grads, (query_heads, grad_heads), row_base, lse_rows, delta_rows)

    def query_chain(step_index, loop_state):
        carried, moving_rows, moving_stats = loop_state
        moving_rows = passed_along(moving_rows, "seq", -1)
        moving_stats = passed_along(moving_stats, "seq", -1)
        carried = query_step(
            carried,
            (moving_rows[0], moving_rows[1]),
            row_base + (step_index + 1) * tok_rows,
            moving_stats[0],
            moving_stats[1],
        )
        return (carried, moving_rows, moving_stats)

    chain_state = lax.fori_loop(
        0,
        span_steps,
        query_chain,
        (first_grads, jnp.stack((query_heads, grad_heads)), jnp.stack((lse_rows, delta_rows))),
    )
    key_grad, value_grad = chain_state[0]
    grad_key = key_grad.reshape(tok_rows, head_count * HEAD_DIM).astype(jnp.bfloat16)
    grad_value = value_grad.reshape(tok_rows, head_count * HEAD_DIM).astype(jnp.bfloat16)
    grad_attn_query, grad_attn_key, grad_attn_value = (
        lax.all_to_all(grad_query, "ch", split_axis=0, concat_axis=1, tiled=True),
        lax.all_to_all(grad_key, "ch", split_axis=0, concat_axis=1, tiled=True),
        lax.all_to_all(grad_value, "ch", split_axis=0, concat_axis=1, tiled=True),
    )
    chan_count = mixer_query.shape[1]
    group_count = conv_filter.shape[0]
    ext_rows = tok_rows + FILTER_LEN
    mixed_input = (mixer_key.astype(jnp.float32) * mixer_value.astype(jnp.float32)).astype(
        jnp.bfloat16
    )
    prior_rows = passed_along(mixed_input[tok_rows - (FILTER_LEN - 1) :], "seq", 1)
    extended = jnp.concatenate(
        (jnp.zeros((1, chan_count), jnp.bfloat16), prior_rows, mixed_input), axis=0
    )
    ext_pos = row_base - FILTER_LEN + jnp.arange(ext_rows, dtype=jnp.int32)
    ext_doc = doc_index(doc_lengths, ext_pos)
    back_mask = ((local_doc[:, None] == ext_doc[None, :]) & (ext_pos[None, :] >= 0)).astype(
        jnp.bfloat16
    )
    reversed_taps = jnp.pad(conv_filter[:, ::-1], ((0, 0), (1, 0)))
    toeplitz = banded(reversed_taps, tok_rows) * back_mask[None]
    ext_groups = extended.reshape(ext_rows, group_count, GROUP)
    conv_out = jnp.einsum(
        "gts,sgc->tgc", toeplitz, ext_groups, preferred_element_type=jnp.float32
    ).reshape(tok_rows, chan_count)
    grad_mixer_query = (mixer_grad.astype(jnp.float32) * conv_out).astype(jnp.bfloat16)
    out_grad = (mixer_grad.astype(jnp.float32) * mixer_query.astype(jnp.float32)).astype(
        jnp.bfloat16
    )
    out_groups = out_grad.reshape(tok_rows, group_count, GROUP)
    block_size = math.gcd(group_count, 16)
    block_count = group_count // block_size
    out_blocks = out_groups.reshape(tok_rows, block_count, block_size, GROUP).transpose(1, 0, 2, 3)
    ext_blocks = ext_groups.reshape(ext_rows, block_count, block_size, GROUP).transpose(1, 0, 2, 3)

    def tap_block(block_parts):
        out_part, ext_part = block_parts
        outer = (
            jnp.einsum("tgc,sgc->gts", out_part, ext_part, preferred_element_type=jnp.float32)
            * back_mask[None]
        )
        return band_sums(outer, FILTER_LEN + 1)

    tap_sums = lax.map(tap_block, (out_blocks, ext_blocks)).reshape(group_count, FILTER_LEN + 1)
    tap_grad = tap_sums[:, 1:][:, ::-1]
    grad_filter = lax.psum(tap_grad, "seq")
    later_rows = passed_along(out_grad[: FILTER_LEN - 1], "seq", -1)
    ahead = jnp.concatenate(
        (out_grad, later_rows, jnp.zeros((1, chan_count), jnp.bfloat16)), axis=0
    ).reshape(ext_rows, group_count, GROUP)
    ahead_pos = row_base + jnp.arange(ext_rows, dtype=jnp.int32)
    ahead_doc = doc_index(doc_lengths, ahead_pos)
    front_mask = (
        (local_doc[:, None] == ahead_doc[None, :]) & (ahead_pos[None, :] < total_tokens)
    ).astype(jnp.bfloat16)
    forward_taps = banded(jnp.pad(conv_filter, ((0, 0), (0, 1))), tok_rows) * front_mask[None]
    input_grad = jnp.einsum(
        "gst,tgc->sgc", forward_taps, ahead, preferred_element_type=jnp.float32
    ).reshape(tok_rows, chan_count)
    grad_mixer_key = (input_grad * mixer_value.astype(jnp.float32)).astype(jnp.bfloat16)
    grad_mixer_value = (input_grad * mixer_key.astype(jnp.float32)).astype(jnp.bfloat16)
    grad_conv_query, grad_conv_key, grad_conv_value = (
        lax.all_to_all(grad_mixer_query, "ch", split_axis=0, concat_axis=1, tiled=True),
        lax.all_to_all(grad_mixer_key, "ch", split_axis=0, concat_axis=1, tiled=True),
        lax.all_to_all(grad_mixer_value, "ch", split_axis=0, concat_axis=1, tiled=True),
    )
    return (
        grad_attn_query,
        grad_attn_key,
        grad_attn_value,
        grad_conv_query,
        grad_conv_key,
        grad_conv_value,
        grad_filter,
    )


def solution(mesh):
    return jax.shard_map(
        body,
        mesh=mesh,
        in_specs=(
            P(("seq", "ch"), None),
            P(("seq", "ch"), None),
            P(("seq", "ch"), None),
            P(("seq", "ch"), None),
            P(("seq", "ch"), None),
            P(("seq", "ch"), None),
            P(("seq", "ch"), None),
            P(("seq", "ch"), None),
            P(("seq", "ch"), None),
            P("ch", None),
            P(),
        ),
        out_specs=(
            P(("seq", "ch"), None),
            P(("seq", "ch"), None),
            P(("seq", "ch"), None),
            P(("seq", "ch"), None),
            P(("seq", "ch"), None),
            P(("seq", "ch"), None),
            P("ch", None),
        ),
        check_vma=False,
    )
```

profile of v0, /device:TPU:0, one launch (start us, length us, event | category | flops | bytes accessed | tf_op | source)
XLA Modules:
  0.0 1128.1 jit_solution(6993194787634608615)
XLA Ops:
  28.9 12.9 %tile.21 = bf16[128,32896]{0,1:T(8,128)(2,1)} reshape(bf16[128,128,257]{0,2,1:T(8,128)(2,1)} %tile.20) | data formatting | bytes 16842752 | tf_op jit(solution)/shard_map/tile | solution.py:31
  41.8 7.1 slice.103
  48.9 12.3 %copy.329 = bf16[128,128,256]{2,1,0:T(8,128)(2,1)} copy(bf16[128,128,256]{0,2,1:T(8,128)(2,1)} %bitcast.247) | data formatting | bytes 16777216 | tf_op jit(solution)/shard_map/reshape | solution.py:32
  65.8 12.9 %tile.9 = bf16[128,32896]{0,1:T(8,128)(2,1)} reshape(bf16[128,128,257]{0,2,1:T(8,128)(2,1)} %tile.8) | data formatting | bytes 16842752 | tf_op jit(solution)/shard_map/tile | solution.py:31
  78.7 7.0 slice.101
  85.7 12.5 %copy.323 = bf16[128,128,256]{2,1,0:T(8,128)(2,1)} copy(bf16[128,128,256]{0,2,1:T(8,128)(2,1)} %bitcast.248) | data formatting | bytes 16777216 | tf_op jit(solution)/shard_map/reshape | solution.py:32
  101.8 5.9 all-to-all-done.1
  111.2 5.9 all-to-all-done.3
  143.5 182.8 %while.60 = (s32[]{:T(128)}, f32[8,128]{1,0:T(8,128)S(1)}, f32[8,128]{1,0:T(8,128)S(1)}, f32[8,128,128]{2,1,0:T(8,128)S(1)}, bf16[2,128,8,128]{3,1,2,0:T(8,128)(...) while((s32[]{:T(128)}, f32[8,128]{1,0:T(8,128)S(1)}, ...), condition=%wide.region_9.10_spmd.clone.clone, body=%wide.region_5.0_spmd.clone.clone.sunk | while | flops 270080896 | bytes 8266233 | solution.py:144
  149.4 11.2 collective-permute-done
  170.6 10.4 collective-permute-done
  184.3 5.8 collective-permute-start
  191.0 9.5 collective-permute-done
  210.4 8.6 collective-permute-done
  222.4 6.2 collective-permute-start
  229.4 7.8 collective-permute-done
  240.5 6.7 collective-permute-start
  248.1 7.0 collective-permute-done
  258.3 6.7 collective-permute-start
  265.9 6.1 collective-permute-done
  275.3 6.7 collective-permute-start
  282.9 6.1 collective-permute-done
  292.3 6.7 collective-permute-start
  299.9 6.1 collective-permute-done
  309.3 6.7 collective-permute-start
  316.8 6.1 collective-permute-done
  356.2 6.9 all-to-all-done.8
  366.3 8.3 collective-permute-start.3
  374.6 224.9 %while.61 = (s32[]{:T(128)}, f32[128,8,128]{2,0,1:T(8,128)S(1)}, f32[128,8,128]{2,0,1:T(8,128)S(1)}, bf16[2,128,8,128]{3,1,2,0:T(8,128)(2,1)}, f32[2,128,8]{1,2,...) while((s32[]{:T(128)}, f32[128,8,128]{2,0,1:T(8,128)S(1)}, ...), condition=%wide.region_12.13_spmd.clone.clone, body=%wide.region_10.12_spmd.clone.clone.sunk | while | flops 470881152 | bytes 9548313 | solution.py:202
  377.5 18.6 %collective-permute-done.1 = f32[2,128,8]{1,2,0:T(8,128)S(1)} collective-permute-done((f32[2,128,8]{1,2,0:T(8,128)S(1)}, f32[2,128,8]{1,2,0:T(8,128)S(1)}, u32[]{:S(2)}, u32[]{:S(2)}) %collective-permute-start.1) | collective-permute-done | bytes 8224 | tf_op jit(solution)/shard_map/while/body/eval_jaxpr/ppermute | solution.py:19
  396.1 10.1 collective-permute-done.2
  417.2 11.6 %collective-permute-done.2 = bf16[2,128,8,128]{3,1,2,0:T(8,128)(2,1)S(1)} collective-permute-done((bf16[2,128,8,128]{3,1,2,0:T(8,128)(2,1)}, bf16[2,128,8,128]{3,1,2,0:T(8,128)(2,1)S(1)}, u32[]{:S(2)}, u32[]{:S(2)}) %collective-permute-start.2) | collective-permute-done | bytes 524320 | tf_op jit(solution)/shard_map/while/body/eval_jaxpr/ppermute | solution.py:19
  439.2 10.7 collective-permute-done.2
  460.4 9.9 collective-permute-done.2
  475.8 7.1 collective-permute-done.1
  482.9 10.0 collective-permute-done.2
  498.5 7.7 collective-permute-done.1
  506.1 9.5 collective-permute-done.2
  521.2 7.7 collective-permute-done.1
  528.8 9.0 collective-permute-done.2
  543.4 7.7 collective-permute-done.1
  551.1 8.5 collective-permute-done.2
  570.5 7.8 collective-permute-done.2
  589.3 7.6 collective-permute-done.2
  643.9 6.0 fusion.27
  661.1 7.9 all-to-all-done.13
  673.5 95.3 %while.59 = (s32[]{:T(128)}, f32[8,16,129]{2,1,0:T(8,128)S(1)}, bf16[8,128,16,16]{1,3,2,0:T(8,128)(2,1)}, bf16[8,256,16,16]{1,3,2,0:T(8,128)(2,1)}, s32[256]{0:T...) while((s32[]{:T(128)}, f32[8,16,129]{2,1,0:T(8,128)S(1)}, ...), condition=%wide.region_17.18_spmd.clone, body=%wide.region_15.17_spmd.clone.sunk | while | flops 17694704 | bytes 20515760 | solution.py:255
  778.3 341.5 %all-reduce.8.cloned.1.call-done = f32[128,128]{1,0:T(8,128)} async-done(((f32[128,128]{1,0:T(8,128)}), f32[128,128]{1,0:T(8,128)}) %all-reduce.8.cloned.1.call-update) | async-done | bytes 65552 | tf_op jit(solution)/shard_map/psum | solution.py:257
  (487 shorter events, 396.0 us)
Async XLA Ops:
  9.0 89.3 %all-to-all-start = ((bf16[32,4,1024]{2,0,1:T(8,128)(2,1)}), bf16[32,4,1024]{2,0,1:T(8,128)(2,1)S(1)}, u32[]{:S(2)}, u32[]{:S(2)}) async-start(bf16[32,4,1024]{2,0,1:T(8,128)(2,1)} %bitcast.201), calls=%async_computation | async-start | bytes 524288 | tf_op jit(solution)/shard_map/all_to_all | solution.py:69
  98.3 9.4 all-to-all-start.1
  107.7 9.4 all-to-all-start.3
  117.1 9.4 all-to-all-start.4
  126.5 9.4 all-to-all-start.2
  135.8 190.4 %all-to-all-start.12 = ((bf16[32,4,2048]{2,0,1:T(8,128)(2,1)}), bf16[32,4,2048]{2,0,1:T(8,128)(2,1)}, u32[]{:S(2)}, u32[]{:S(2)}) async-start(bf16[32,4,2048]{2,0,1:T(8,128)(2,1)} %bitcast.193), calls=%async_computation.12 | async-start | bytes 1048576 | tf_op jit(solution)/shard_map/all_to_all | solution.py:74
  143.5 17.1 %collective-permute-start = (bf16[2,128,8,128]{3,1,2,0:T(8,128)(2,1)}, bf16[2,128,8,128]{3,1,2,0:T(8,128)(2,1)S(1)}, u32[]{:S(2)}, u32[]{:S(2)}) collective-permute-start(bf16[2,128,8,128]{3,1,2,0:T(8,128)(2,1)} %get-tuple-element.1174), channel_id=1, source_target_pairs={{0,4},{4,8},{8,12},{12,16},{16,20},{20,24},{24,28},{28,32},{32,36}... | collective-permute-start | bytes 1572872 | tf_op jit(solution)/shard_map/while/body/eval_jaxpr/ppermute | solution.py:19
  163.9 17.0 %collective-permute-start = (bf16[2,128,8,128]{3,1,2,0:T(8,128)(2,1)}, bf16[2,128,8,128]{3,1,2,0:T(8,128)(2,1)S(1)}, u32[]{:S(2)}, u32[]{:S(2)}) collective-permute-start(bf16[2,128,8,128]{3,1,2,0:T(8,128)(2,1)} %get-tuple-element.1174), channel_id=1, source_target_pairs={{0,4},{4,8},{8,12},{12,16},{16,20},{20,24},{24,28},{28,32},{32,36}... | collective-permute-start | bytes 1572872 | tf_op jit(solution)/shard_map/while/body/eval_jaxpr/ppermute | solution.py:19
  184.3 16.2 %collective-permute-start = (bf16[2,128,8,128]{3,1,2,0:T(8,128)(2,1)}, bf16[2,128,8,128]{3,1,2,0:T(8,128)(2,1)S(1)}, u32[]{:S(2)}, u32[]{:S(2)}) collective-permute-start(bf16[2,128,8,128]{3,1,2,0:T(8,128)(2,1)} %get-tuple-element.1174), channel_id=1, source_target_pairs={{0,4},{4,8},{8,12},{12,16},{16,20},{20,24},{24,28},{28,32},{32,36}... | collective-permute-start | bytes 1572872 | tf_op jit(solution)/shard_map/while/body/eval_jaxpr/ppermute | solution.py:19
  203.7 15.3 %collective-permute-start = (bf16[2,128,8,128]{3,1,2,0:T(8,128)(2,1)}, bf16[2,128,8,128]{3,1,2,0:T(8,128)(2,1)S(1)}, u32[]{:S(2)}, u32[]{:S(2)}) collective-permute-start(bf16[2,128,8,128]{3,1,2,0:T(8,128)(2,1)} %get-tuple-element.1174), channel_id=1, source_target_pairs={{0,4},{4,8},{8,12},{12,16},{16,20},{20,24},{24,28},{28,32},{32,36}... | collective-permute-start | bytes 1572872 | tf_op jit(solution)/shard_map/while/body/eval_jaxpr/ppermute | solution.py:19
  222.4 14.9 %collective-permute-start = (bf16[2,128,8,128]{3,1,2,0:T(8,128)(2,1)}, bf16[2,128,8,128]{3,1,2,0:T(8,128)(2,1)S(1)}, u32[]{:S(2)}, u32[]{:S(2)}) collective-permute-start(bf16[2,128,8,128]{3,1,2,0:T(8,128)(2,1)} %get-tuple-element.1174), channel_id=1, source_target_pairs={{0,4},{4,8},{8,12},{12,16},{16,20},{20,24},{24,28},{28,32},{32,36}... | collective-permute-start | bytes 1572872 | tf_op jit(solution)/shard_map/while/body/eval_jaxpr/ppermute | solution.py:19
  240.5 14.5 %collective-permute-start = (bf16[2,128,8,128]{3,1,2,0:T(8,128)(2,1)}, bf16[2,128,8,128]{3,1,2,0:T(8,128)(2,1)S(1)}, u32[]{:S(2)}, u32[]{:S(2)}) collective-permute-start(bf16[2,128,8,128]{3,1,2,0:T(8,128)(2,1)} %get-tuple-element.1174), channel_id=1, source_target_pairs={{0,4},{4,8},{8,12},{12,16},{16,20},{20,24},{24,28},{28,32},{32,36}... | collective-permute-start | bytes 1572872 | tf_op jit(solution)/shard_map/while/body/eval_jaxpr/ppermute | solution.py:19
  258.3 13.7 %collective-permute-start = (bf16[2,128,8,128]{3,1,2,0:T(8,128)(2,1)}, bf16[2,128,8,128]{3,1,2,0:T(8,128)(2,1)S(1)}, u32[]{:S(2)}, u32[]{:S(2)}) collective-permute-start(bf16[2,128,8,128]{3,1,2,0:T(8,128)(2,1)} %get-tuple-element.1174), channel_id=1, source_target_pairs={{0,4},{4,8},{8,12},{12,16},{16,20},{20,24},{24,28},{28,32},{32,36}... | collective-permute-start | bytes 1572872 | tf_op jit(solution)/shard_map/while/body/eval_jaxpr/ppermute | solution.py:19
  275.3 13.7 %collective-permute-start = (bf16[2,128,8,128]{3,1,2,0:T(8,128)(2,1)}, bf16[2,128,8,128]{3,1,2,0:T(8,128)(2,1)S(1)}, u32[]{:S(2)}, u32[]{:S(2)}) collective-permute-start(bf16[2,128,8,128]{3,1,2,0:T(8,128)(2,1)} %get-tuple-element.1174), channel_id=1, source_target_pairs={{0,4},{4,8},{8,12},{12,16},{16,20},{20,24},{24,28},{28,32},{32,36}... | collective-permute-start | bytes 1572872 | tf_op jit(solution)/shard_map/while/body/eval_jaxpr/ppermute | solution.py:19
  292.3 13.7 %collective-permute-start = (bf16[2,128,8,128]{3,1,2,0:T(8,128)(2,1)}, bf16[2,128,8,128]{3,1,2,0:T(8,128)(2,1)S(1)}, u32[]{:S(2)}, u32[]{:S(2)}) collective-permute-start(bf16[2,128,8,128]{3,1,2,0:T(8,128)(2,1)} %get-tuple-element.1174), channel_id=1, source_target_pairs={{0,4},{4,8},{8,12},{12,16},{16,20},{20,24},{24,28},{28,32},{32,36}... | collective-permute-start | bytes 1572872 | tf_op jit(solution)/shard_map/while/body/eval_jaxpr/ppermute | solution.py:19
  309.3 13.7 %collective-permute-start = (bf16[2,128,8,128]{3,1,2,0:T(8,128)(2,1)}, bf16[2,128,8,128]{3,1,2,0:T(8,128)(2,1)S(1)}, u32[]{:S(2)}, u32[]{:S(2)}) collective-permute-start(bf16[2,128,8,128]{3,1,2,0:T(8,128)(2,1)} %get-tuple-element.1174), channel_id=1, source_target_pairs={{0,4},{4,8},{8,12},{12,16},{16,20},{20,24},{24,28},{28,32},{32,36}... | collective-permute-start | bytes 1572872 | tf_op jit(solution)/shard_map/while/body/eval_jaxpr/ppermute | solution.py:19
  326.3 12.3 %all-to-all-start.9 = ((bf16[32,4,2048]{2,0,1:T(8,128)(2,1)}), bf16[32,4,2048]{2,0,1:T(8,128)(2,1)S(1)}, u32[]{:S(2)}, u32[]{:S(2)}) async-start(bf16[32,4,2048]{2,0,1:T(8,128)(2,1)} %bitcast.270), calls=%async_computation.9 | async-start | bytes 1048576 | tf_op jit(solution)/shard_map/all_to_all | solution.py:75
  338.5 12.3 %all-to-all-start.10 = ((bf16[32,4,2048]{2,0,1:T(8,128)(2,1)}), bf16[32,4,2048]{2,0,1:T(8,128)(2,1)S(1)}, u32[]{:S(2)}, u32[]{:S(2)}) async-start(bf16[32,4,2048]{2,0,1:T(8,128)(2,1)} %bitcast.269), calls=%async_computation.10 | async-start | bytes 1048576 | tf_op jit(solution)/shard_map/all_to_all | solution.py:76
  350.8 12.3 %all-to-all-start.8 = ((bf16[32,4,2048]{2,0,1:T(8,128)(2,1)}), bf16[32,4,2048]{2,0,1:T(8,128)(2,1)S(1)}, u32[]{:S(2)}, u32[]{:S(2)}) async-start(bf16[32,4,2048]{2,0,1:T(8,128)(2,1)} %bitcast.268), calls=%async_computation.8 | async-start | bytes 1048576 | tf_op jit(solution)/shard_map/all_to_all | solution.py:77
  365.0 246.0 %collective-permute-start.4 = (bf16[127,2048]{1,0:T(8,128)(2,1)}, bf16[127,2048]{1,0:T(8,128)(2,1)}, u32[]{:S(2)}, u32[]{:S(2)}) collective-permute-start(bf16[127,2048]{1,0:T(8,128)(2,1)} %bitcast.202), channel_id=1, source_target_pairs={{4,0},{8,4},{12,8},{16,12},{20,16},{24,20},{28,24},{32,28},{36,32}... | collective-permute-start | bytes 1560584 | tf_op jit(solution)/shard_map/ppermute | solution.py:19
  366.3 244.7 %collective-permute-start.3 = (bf16[127,2048]{1,0:T(8,128)(2,1)}, bf16[127,2048]{1,0:T(8,128)(2,1)}, u32[]{:S(2)}, u32[]{:S(2)}) collective-permute-start(bf16[127,2048]{1,0:T(8,128)(2,1)} %slice.100), channel_id=1, source_target_pairs={{0,4},{4,8},{8,12},{12,16},{16,20},{20,24},{24,28},{28,32},{32,36}... | collective-permute-start | bytes 1560584 | tf_op jit(solution)/shard_map/ppermute | solution.py:19
  374.6 21.5 %collective-permute-start.1 = (f32[2,128,8]{1,2,0:T(8,128)S(1)}, f32[2,128,8]{1,2,0:T(8,128)S(1)}, u32[]{:S(2)}, u32[]{:S(2)}) collective-permute-start(f32[2,128,8]{1,2,0:T(8,128)S(1)} %get-tuple-element.1212), channel_id=1, source_target_pairs={{4,0},{8,4},{12,8},{16,12},{20,16},{24,20},{28,24},{32,28},{36,32}... | collective-permute-start | bytes 24584 | tf_op jit(solution)/shard_map/while/body/eval_jaxpr/ppermute | solution.py:19
  375.9 30.3 %collective-permute-start.2 = (bf16[2,128,8,128]{3,1,2,0:T(8,128)(2,1)}, bf16[2,128,8,128]{3,1,2,0:T(8,128)(2,1)S(1)}, u32[]{:S(2)}, u32[]{:S(2)}) collective-permute-start(bf16[2,128,8,128]{3,1,2,0:T(8,128)(2,1)} %get-tuple-element.1211), channel_id=1, source_target_pairs={{4,0},{8,4},{12,8},{16,12},{20,16},{24,20},{28,24},{32,28},{36,32}... | collective-permute-start | bytes 1572872 | tf_op jit(solution)/shard_map/while/body/eval_jaxpr/ppermute | solution.py:19
  408.9 8.3 collective-permute-start.1
  410.2 18.6 %collective-permute-start.2 = (bf16[2,128,8,128]{3,1,2,0:T(8,128)(2,1)}, bf16[2,128,8,128]{3,1,2,0:T(8,128)(2,1)S(1)}, u32[]{:S(2)}, u32[]{:S(2)}) collective-permute-start(bf16[2,128,8,128]{3,1,2,0:T(8,128)(2,1)} %get-tuple-element.1211), channel_id=1, source_target_pairs={{4,0},{8,4},{12,8},{16,12},{20,16},{24,20},{28,24},{32,28},{36,32}... | collective-permute-start | bytes 1572872 | tf_op jit(solution)/shard_map/while/body/eval_jaxpr/ppermute | solution.py:19
  431.5 7.8 collective-permute-start.1
  432.8 17.2 %collective-permute-start.2 = (bf16[2,128,8,128]{3,1,2,0:T(8,128)(2,1)}, bf16[2,128,8,128]{3,1,2,0:T(8,128)(2,1)S(1)}, u32[]{:S(2)}, u32[]{:S(2)}) collective-permute-start(bf16[2,128,8,128]{3,1,2,0:T(8,128)(2,1)} %get-tuple-element.1211), channel_id=1, source_target_pairs={{4,0},{8,4},{12,8},{16,12},{20,16},{24,20},{28,24},{32,28},{36,32}... | collective-permute-start | bytes 1572872 | tf_op jit(solution)/shard_map/while/body/eval_jaxpr/ppermute | solution.py:19
  452.6 7.8 collective-permute-start.1
  453.9 16.4 %collective-permute-start.2 = (bf16[2,128,8,128]{3,1,2,0:T(8,128)(2,1)}, bf16[2,128,8,128]{3,1,2,0:T(8,128)(2,1)S(1)}, u32[]{:S(2)}, u32[]{:S(2)}) collective-permute-start(bf16[2,128,8,128]{3,1,2,0:T(8,128)(2,1)} %get-tuple-element.1211), channel_id=1, source_target_pairs={{4,0},{8,4},{12,8},{16,12},{20,16},{24,20},{28,24},{32,28},{36,32}... | collective-permute-start | bytes 1572872 | tf_op jit(solution)/shard_map/while/body/eval_jaxpr/ppermute | solution.py:19
  473.0 9.9 collective-permute-start.1
  474.3 18.6 %collective-permute-start.2 = (bf16[2,128,8,128]{3,1,2,0:T(8,128)(2,1)}, bf16[2,128,8,128]{3,1,2,0:T(8,128)(2,1)S(1)}, u32[]{:S(2)}, u32[]{:S(2)}) collective-permute-start(bf16[2,128,8,128]{3,1,2,0:T(8,128)(2,1)} %get-tuple-element.1211), channel_id=1, source_target_pairs={{4,0},{8,4},{12,8},{16,12},{20,16},{24,20},{28,24},{32,28},{36,32}... | collective-permute-start | bytes 1572872 | tf_op jit(solution)/shard_map/while/body/eval_jaxpr/ppermute | solution.py:19
  495.6 10.5 collective-permute-start.1
  496.9 18.7 %collective-permute-start.2 = (bf16[2,128,8,128]{3,1,2,0:T(8,128)(2,1)}, bf16[2,128,8,128]{3,1,2,0:T(8,128)(2,1)S(1)}, u32[]{:S(2)}, u32[]{:S(2)}) collective-permute-start(bf16[2,128,8,128]{3,1,2,0:T(8,128)(2,1)} %get-tuple-element.1211), channel_id=1, source_target_pairs={{4,0},{8,4},{12,8},{16,12},{20,16},{24,20},{28,24},{32,28},{36,32}... | collective-permute-start | bytes 1572872 | tf_op jit(solution)/shard_map/while/body/eval_jaxpr/ppermute | solution.py:19
  518.3 10.5 collective-permute-start.1
  519.6 18.2 %collective-permute-start.2 = (bf16[2,128,8,128]{3,1,2,0:T(8,128)(2,1)}, bf16[2,128,8,128]{3,1,2,0:T(8,128)(2,1)S(1)}, u32[]{:S(2)}, u32[]{:S(2)}) collective-permute-start(bf16[2,128,8,128]{3,1,2,0:T(8,128)(2,1)} %get-tuple-element.1211), channel_id=1, source_target_pairs={{4,0},{8,4},{12,8},{16,12},{20,16},{24,20},{28,24},{32,28},{36,32}... | collective-permute-start | bytes 1572872 | tf_op jit(solution)/shard_map/while/body/eval_jaxpr/ppermute | solution.py:19
  540.6 10.5 collective-permute-start.1
  541.9 17.8 %collective-permute-start.2 = (bf16[2,128,8,128]{3,1,2,0:T(8,128)(2,1)}, bf16[2,128,8,128]{3,1,2,0:T(8,128)(2,1)S(1)}, u32[]{:S(2)}, u32[]{:S(2)}) collective-permute-start(bf16[2,128,8,128]{3,1,2,0:T(8,128)(2,1)} %get-tuple-element.1211), channel_id=1, source_target_pairs={{4,0},{8,4},{12,8},{16,12},{20,16},{24,20},{28,24},{32,28},{36,32}... | collective-permute-start | bytes 1572872 | tf_op jit(solution)/shard_map/while/body/eval_jaxpr/ppermute | solution.py:19
  562.3 8.2 collective-permute-start.1
  563.6 14.7 %collective-permute-start.2 = (bf16[2,128,8,128]{3,1,2,0:T(8,128)(2,1)}, bf16[2,128,8,128]{3,1,2,0:T(8,128)(2,1)S(1)}, u32[]{:S(2)}, u32[]{:S(2)}) collective-permute-start(bf16[2,128,8,128]{3,1,2,0:T(8,128)(2,1)} %get-tuple-element.1211), channel_id=1, source_target_pairs={{4,0},{8,4},{12,8},{16,12},{20,16},{24,20},{28,24},{32,28},{36,32}... | collective-permute-start | bytes 1572872 | tf_op jit(solution)/shard_map/while/body/eval_jaxpr/ppermute | solution.py:19
  581.0 8.3 collective-permute-start.1
  582.3 14.6 %collective-permute-start.2 = (bf16[2,128,8,128]{3,1,2,0:T(8,128)(2,1)}, bf16[2,128,8,128]{3,1,2,0:T(8,128)(2,1)S(1)}, u32[]{:S(2)}, u32[]{:S(2)}) collective-permute-start(bf16[2,128,8,128]{3,1,2,0:T(8,128)(2,1)} %get-tuple-element.1211), channel_id=1, source_target_pairs={{4,0},{8,4},{12,8},{16,12},{20,16},{24,20},{28,24},{32,28},{36,32}... | collective-permute-start | bytes 1572872 | tf_op jit(solution)/shard_map/while/body/eval_jaxpr/ppermute | solution.py:19
  600.6 13.9 %all-to-all-start.7 = ((bf16[4,32,1024]{2,1,0:T(8,128)(2,1)}), bf16[4,32,1024]{2,1,0:T(8,128)(2,1)S(1)}, u32[]{:S(2)}, u32[]{:S(2)}) async-start(bf16[4,32,1024]{2,1,0:T(8,128)(2,1)} %convert_element_type.208), calls=%async_computation.7 | async-start | bytes 524288 | tf_op jit(solution)/shard_map/all_to_all | solution.py:214
  614.5 16.5 %all-to-all-start.5 = ((bf16[4,32,1024]{2,1,0:T(8,128)(2,1)}), bf16[4,32,1024]{2,1,0:T(8,128)(2,1)}, u32[]{:S(2)}, u32[]{:S(2)}) async-start(bf16[4,32,1024]{2,1,0:T(8,128)(2,1)} %convert_element_type.204), calls=%async_computation.5 | async-start | bytes 524288 | tf_op jit(solution)/shard_map/all_to_all | solution.py:212
  631.0 9.4 all-to-all-start.6
  640.4 16.2 %all-to-all-start.14 = ((bf16[4,32,2048]{2,1,0:T(8,128)(2,1)}), bf16[4,32,2048]{2,1,0:T(8,128)(2,1)S(1)}, u32[]{:S(2)}, u32[]{:S(2)}) async-start(bf16[4,32,2048]{2,1,0:T(8,128)(2,1)} %get-tuple-element.946), calls=%async_computation.14 | async-start | bytes 1048576 | tf_op jit(solution)/shard_map/all_to_all | solution.py:276
  656.6 12.4 %all-to-all-start.13 = ((bf16[4,32,2048]{2,1,0:T(8,128)(2,1)}), bf16[4,32,2048]{2,1,0:T(8,128)(2,1)S(1)}, u32[]{:S(2)}, u32[]{:S(2)}) async-start(bf16[4,32,2048]{2,1,0:T(8,128)(2,1)} %get-tuple-element.947), calls=%async_computation.13 | async-start | bytes 1048576 | tf_op jit(solution)/shard_map/all_to_all | solution.py:275
  669.0 107.4 %all-to-all-start.11 = ((bf16[4,32,2048]{2,1,0:T(8,128)(2,1)}), bf16[4,32,2048]{2,1,0:T(8,128)(2,1)}, u32[]{:S(2)}, u32[]{:S(2)}) async-start(bf16[4,32,2048]{2,1,0:T(8,128)(2,1)} %fusion.40), calls=%async_computation.11 | async-start | bytes 1048576 | tf_op jit(solution)/shard_map/all_to_all | solution.py:274
  673.2 446.6 %all-reduce.8.cloned.1.call-start = ((), (), s32[]{:S(2)}) async-start(), calls=%async_computation.15 | async-start | bytes 131072 | tf_op jit(solution)/shard_map/psum | solution.py:257
  (23 other events, 425.4 us)
Sparse Core Ops, SparseCore 0:
  769.8 349.9 all-reduce.7
where the time goes:
time: 1130 us
  waiting for transfers between devices  638 us (56%)
  local copies, waits for them, and re-layouts  225 us (20%)
  starting transfers between devices  153 us (14%)
  matrix products  70.3 us (6%)
  other arithmetic  24.6 us (2%)
  between operations  14.7 us (1%)
    psum x1, waiting for transfers between devices, body(): grad_filter = lax.psum(tap_grad, 'seq')  341 us
    ppermute x32, waiting for transfers between devices, passed_along(): return lax.ppermute(block, axis, route)  248 us
    ppermute x32, starting transfers between devices, passed_along(): return lax.ppermute(block, axis, route)  97.7 us
    another operation x4, local copies, waits for them, and re-layouts, banded(): repeated = jnp.tile(padded, (1, row_count))[:, :row_count * span_count]  34.8 us
    reshape x8, local copies, waits for them, and re-layouts, band_sums(): skewed = flattened.reshape(group_count, row_count, span_count + 2)  33.9 us
    reshape x2, local copies, waits for them, and re-layouts, banded(): return repeated.reshape(group_count, row_count, span_count)  24.9 us
    pad x8, local copies, waits for them, and re-layouts, band_sums(): jnp.pad(padded.reshape(group_count, row_count * (span_count + 1)), ((0, 0...  24.8 us
  transfers between devices with their start and end apart: 48, of which 40 were waited for; matrix products, arithmetic and copies ran while one was open for 28% of the time, Pallas kernels for 0%

commit v1 on v0

v1 whole, which is shorter than its diff:
```python
import functools
import math

import jax
import jax.numpy as jnp
from jax import lax
from jax.experimental import pallas as pl
from jax.experimental.pallas import tpu as pltpu
from jax.sharding import PartitionSpec as P

MESH = pl.DeviceIdType.MESH
HEAD_DIM = 128
FILTER_LEN = 128
DOCS = 12
PLANE = 32
PLANES = 4
ROWS = 32
SPAN = PLANE * ROWS
TILE = 256
NEAR = SPAN // TILE
REACH = 5
WINDOW = SPAN + REACH * TILE
CONV_WIDTH = 256
CONV_GROUPS = 16
LOG2_SCALE = math.log2(math.e) / math.sqrt(HEAD_DIM)
SCALE = 1.0 / math.sqrt(HEAD_DIM)
NEG_FILL = -1e30
VMEM_LIMIT = 60 * 1024 * 1024


def place_in_slice():
    me = lax.axis_index("seq") * 4 + lax.axis_index("ch")
    return lax.div(me, PLANE), lax.rem(me, PLANE)


def device_of(z, p):
    return (z * (PLANE // 4) + lax.div(p, 4), lax.rem(p, 4))


def conv_block(p):
    return lax.rem(p, 4) * (PLANE // 4) + lax.div(p, 4)


def greet(z, p):
    barrier = pltpu.get_barrier_semaphore()

    def hello(k, carried):
        pl.semaphore_signal(
            barrier, inc=1, device_id=device_of(z, lax.rem(p + k, PLANE)), device_id_type=MESH
        )
        return carried

    lax.fori_loop(1, PLANE, hello, 0)
    for step in range(1, PLANES):
        pl.semaphore_signal(
            barrier, inc=1, device_id=device_of(lax.rem(z + step, PLANES), p), device_id_type=MESH
        )
    pl.semaphore_wait(barrier, PLANE - 1 + PLANES - 1)


def wait_bytes(ref, sem):
    pltpu.make_async_copy(ref, ref, sem).wait()


def spread_kernel(
    q, k, v, o, g, mix, og, qw, kw, vw, ow, gw, mw, ogw, send_sem, recv_sem, zsend_sem, zrecv_sem
):
    z, p = place_in_slice()
    greet(z, p)

    def send(slot, src, dst, base, width, block):
        mine = dst.at[pl.ds(pl.multiple_of(base + p * ROWS, ROWS), ROWS), :]

        def columns(r):
            return src.at[:, pl.ds(pl.multiple_of(block(r) * width, width), width)]

        pltpu.make_async_copy(columns(p), mine, recv_sem.at[slot]).start()

        def step(i, carried):
            r = lax.rem(p + i, PLANE)
            pltpu.make_async_remote_copy(
                src_ref=columns(r),
                dst_ref=mine,
                send_sem=send_sem.at[slot],
                recv_sem=recv_sem.at[slot],
                device_id=device_of(z, r),
                device_id_type=MESH,
            ).start()
            return carried

        lax.fori_loop(1, PLANE, step, 0)

    hops = []

    def hop(slot, ref, src_row, dst_row, count, step):
        copy = pltpu.make_async_remote_copy(
            src_ref=ref.at[pl.ds(src_row, count), :],
            dst_ref=ref.at[pl.ds(dst_row, count), :],
            send_sem=zsend_sem.at[slot],
            recv_sem=zrecv_sem.at[slot],
            device_id=device_of(lax.rem(z + step, PLANES), p),
            device_id_type=MESH,
        )
        copy.start()
        hops.append(copy)

    def arrived(slot, dst, base):
        wait_bytes(dst.at[pl.ds(base, SPAN), :], recv_sem.at[slot])

    head = lambda r: r
    back = REACH * TILE
    send(0, k, kw, back, HEAD_DIM, head)
    send(1, v, vw, back, HEAD_DIM, head)
    send(2, q, qw, 0, HEAD_DIM, head)
    send(3, g, gw, 0, HEAD_DIM, head)
    for slot, ref in ((0, kw), (1, vw)):
        arrived(slot, ref, back)
        hop(2 * slot, ref, back, TILE, SPAN, 1)
        hop(2 * slot + 1, ref, SPAN + back - TILE, 0, TILE, 2)
    send(5, mix, mw, FILTER_LEN, CONV_WIDTH, conv_block)
    for slot, ref in ((2, qw), (3, gw)):
        arrived(slot, ref, 0)
        hop(2 * slot, ref, 0, SPAN, SPAN, 3)
        hop(2 * slot + 1, ref, 0, 2 * SPAN, TILE, 2)
    send(6, og, ogw, 0, CONV_WIDTH, conv_block)
    send(4, o, ow, 0, HEAD_DIM, head)
    arrived(5, mw, FILTER_LEN)
    hop(8, mw, SPAN, 0, FILTER_LEN, 1)
    arrived(6, ogw, 0)
    hop(9, ogw, 0, SPAN, FILTER_LEN, 3)
    arrived(4, ow, 0)
    rest = SPAN - ROWS
    for slot, ref in enumerate((kw, vw, qw, gw, ow, mw, ogw)):
        wait_bytes(ref.at[pl.ds(0, rest), :], send_sem.at[slot])
    for copy in hops:
        copy.wait()


def spread(q, k, v, o, g, mix, og):
    bf16 = jnp.bfloat16
    any_space = pl.BlockSpec(memory_space=pl.ANY)
    window = jax.ShapeDtypeStruct((WINDOW, HEAD_DIM), bf16)
    conv = jax.ShapeDtypeStruct((SPAN + FILTER_LEN, CONV_WIDTH), bf16)
    return pl.pallas_call(
        spread_kernel,
        out_shape=(
            window,
            window,
            window,
            jax.ShapeDtypeStruct((SPAN, HEAD_DIM), bf16),
            window,
            conv,
            conv,
        ),
        in_specs=[any_space] * 7,
        out_specs=(any_space,) * 7,
        scratch_shapes=[
            pltpu.SemaphoreType.DMA((7,)),
            pltpu.SemaphoreType.DMA((7,)),
            pltpu.SemaphoreType.DMA((10,)),
            pltpu.SemaphoreType.DMA((10,)),
        ],
        compiler_params=pltpu.CompilerParams(collective_id=0, has_side_effects=True),
        name="spread",
    )(q, k, v, o, g, mix, og)


def doc_ends(len_ref):
    ends = []
    total = jnp.int32(0)
    for d in range(DOCS):
        total = total + len_ref[d]
        ends.append(total)
    return ends


def doc_start(ends, pos):
    start = jnp.zeros_like(pos)
    for end in ends:
        start = jnp.maximum(start, jnp.where(end <= pos, end, 0))
    return start


def doc_stop(ends, pos):
    stop = jnp.full_like(pos, ends[-1])
    for end in ends:
        stop = jnp.minimum(stop, jnp.where(end > pos, end, ends[-1]))
    return stop


def nt_dot(a, b):
    return lax.dot_general(a, b, (((1,), (1,)), ((), ())), preferred_element_type=jnp.float32)


def tile_rows(ref, i):
    return ref[pl.ds(pl.multiple_of(i * TILE, TILE), TILE), :]


def row_positions(base):
    return base + lax.broadcasted_iota(jnp.int32, (1, TILE), 1)


def first_tile(ends, z, q_base):
    start = doc_start(ends, q_base)
    return lax.div(start - (z * SPAN - REACH * TILE), TILE)


def seen_before(z, kb, starts):
    k_pos = z * SPAN - REACH * TILE + kb * TILE + lax.broadcasted_iota(jnp.int32, (TILE, TILE), 0)
    return k_pos >= starts


def seen_diagonal(z, kb, starts):
    below = lax.broadcasted_iota(jnp.int32, (TILE, TILE), 0) <= lax.broadcasted_iota(
        jnp.int32, (TILE, TILE), 1
    )
    return seen_before(z, kb, starts) & below


def stats_kernel(len_ref, qw, kw, gw, ow, out_ref):
    z, _ = place_in_slice()
    ends = doc_ends(len_ref)

    def query_tile(qi, carried):
        q_base = z * SPAN + qi * TILE
        starts = doc_start(ends, row_positions(q_base))
        query = tile_rows(qw, qi)

        def scores(kb, seen):
            s = nt_dot(tile_rows(kw, kb), query) * LOG2_SCALE
            return jnp.where(seen(z, kb, starts), s, NEG_FILL)

        s = scores(qi + REACH, seen_diagonal)
        top = jnp.max(s, axis=0, keepdims=True)
        total = jnp.sum(jnp.exp2(s - top), axis=0, keepdims=True)

        def key_tile(kb, state):
            top, total = state
            s = scores(kb, seen_before)
            new_top = jnp.maximum(top, jnp.max(s, axis=0, keepdims=True))
            total = total * jnp.exp2(top - new_top) + jnp.sum(
                jnp.exp2(s - new_top), axis=0, keepdims=True
            )
            return new_top, total

        top, total = lax.fori_loop(
            first_tile(ends, z, q_base), qi + REACH, key_tile, (top, total)
        )
        product = tile_rows(gw, qi).astype(jnp.float32) * tile_rows(ow, qi).astype(jnp.float32)
        out_ref[qi, 0:1, :] = top + jnp.log2(total)
        out_ref[qi, 1:2, :] = jnp.sum(product.T, axis=0, keepdims=True)
        return carried

    lax.fori_loop(0, NEAR, query_tile, 0)


def grads_kernel(
    len_ref, qw, kw, vw, gw, own_stats, near_stats, far_stats, dq, dk, dv, stats, dk_sum, dv_sum, dq_sum
):
    z, _ = place_in_slice()
    ends = doc_ends(len_ref)
    stats[0:NEAR] = own_stats[...]
    stats[NEAR : 2 * NEAR] = near_stats[...]
    stats[2 * NEAR : 2 * NEAR + 1] = far_stats[...]
    dk_sum[...] = jnp.zeros_like(dk_sum)
    dv_sum[...] = jnp.zeros_like(dv_sum)

    def pair(qi, kb, starts, seen, for_query, for_key):
        query = tile_rows(qw, qi)
        grad = tile_rows(gw, qi)
        key = tile_rows(kw, kb)
        s = nt_dot(key, query) * LOG2_SCALE - stats[qi, 0:1, :]
        probs = jnp.where(seen(z, kb, starts), jnp.exp2(s), 0.0)
        grad_scores = probs * (nt_dot(tile_rows(vw, kb), grad) - stats[qi, 1:2, :])
        grad_scores = grad_scores.astype(jnp.bfloat16)
        if for_key:
            rows = pl.ds(pl.multiple_of((kb - REACH) * TILE, TILE), TILE)
            dv_sum[rows, :] += jnp.dot(
                probs.astype(jnp.bfloat16), grad, preferred_element_type=jnp.float32
            )
            dk_sum[rows, :] += jnp.dot(grad_scores, query, preferred_element_type=jnp.float32)
        if for_query:
            dq_sum[...] += lax.dot_general(
                key, grad_scores, (((0,), (0,)), ((), ())), preferred_element_type=jnp.float32
            )

    def own_tile(qi, carried):
        q_base = z * SPAN + qi * TILE
        starts = doc_start(ends, row_positions(q_base))
        first = first_tile(ends, z, q_base)
        dq_sum[...] = jnp.zeros_like(dq_sum)

        def before(kb, inner):
            pair(qi, kb, starts, seen_before, True, False)
            return inner

        def within(kb, inner):
            pair(qi, kb, starts, seen_before, True, True)
            return inner

        lax.fori_loop(first, REACH, before, 0)
        lax.fori_loop(jnp.maximum(first, REACH), REACH + qi, within, 0)
        pair(qi, REACH + qi, starts, seen_diagonal, True, True)
        rows = pl.ds(pl.multiple_of(qi * TILE, TILE), TILE)
        dq[rows, :] = (dq_sum[...].T * SCALE).astype(jnp.bfloat16)
        return carried

    lax.fori_loop(0, NEAR, own_tile, 0)

    def later_tile(qi, carried):
        q_base = z * SPAN + qi * TILE
        starts = doc_start(ends, row_positions(q_base))

        def after(kb, inner):
            pair(qi, kb, starts, seen_before, False, True)
            return inner

        first = jnp.maximum(first_tile(ends, z, q_base), REACH)
        lax.fori_loop(first, REACH + NEAR, after, 0)
        return carried

    lax.fori_loop(NEAR, NEAR + REACH, later_tile, 0)
    dk[...] = (dk_sum[...] * SCALE).astype(jnp.bfloat16)
    dv[...] = dv_sum[...].astype(jnp.bfloat16)


def conv_kernel(len_ref, taps, back_taps, mw, ogw, out_ref, grad_ref, tap_ref, circ, back_circ, tap_sum):
    z, _ = place_in_slice()
    ends = doc_ends(len_ref)
    size = FILTER_LEN
    bf16 = jnp.bfloat16
    for group in range(CONV_GROUPS):
        for src, dst in ((taps, circ), (back_taps, back_circ)):
            row = jnp.broadcast_to(src[group : group + 1, :], (size, size))
            dst[group] = pltpu.roll(row, 0, 1, stride=1, stride_axis=0).astype(bf16)
    tap_sum[...] = jnp.zeros_like(tap_sum)
    down = lax.broadcasted_iota(jnp.int32, (size, size), 0)
    across = lax.broadcasted_iota(jnp.int32, (size, size), 1)
    group_of_lane = lax.div(across, 16)

    def block(tb, carried):
        base = z * SPAN + tb * size
        positions = base + lax.broadcasted_iota(jnp.int32, (1, size), 1)

        def as_column(row):
            return jnp.broadcast_to(row.astype(jnp.float32), (size, size)).T.astype(jnp.int32)

        start = as_column(doc_start(ends, positions))
        stop = as_column(doc_stop(ends, positions))
        prev = jnp.where((across > down) & (base - size + across >= start), 1.0, 0.0)
        here = jnp.where((across <= down) & (base + across >= start), 1.0, 0.0)
        ahead = jnp.where((across >= down) & (base + across < stop), 1.0, 0.0)
        beyond = jnp.where((across < down) & (base + size + across < stop), 1.0, 0.0)
        prev_b, here_b = prev.astype(bf16), here.astype(bf16)
        ahead_b, beyond_b = ahead.astype(bf16), beyond.astype(bf16)
        rows = pl.ds(pl.multiple_of(tb * size, size), size)
        both = pl.ds(pl.multiple_of(tb * size, size), 2 * size)
        for half in range(2):
            lanes = slice(half * 128, half * 128 + 128)
            mixed = mw[both, lanes]
            grads = ogw[both, lanes]
            own = ogw[rows, lanes]
            out = jnp.zeros((size, size), jnp.float32)
            back = jnp.zeros((size, size), jnp.float32)
            for member in range(8):
                group = half * 8 + member
                chosen = group_of_lane == member
                band = back_circ[group]
                out = jnp.where(
                    chosen,
                    jnp.dot(
                        jnp.concatenate((band * prev_b, band * here_b), axis=1),
                        mixed,
                        preferred_element_type=jnp.float32,
                    ),
                    out,
                )
                band = circ[group]
                back = jnp.where(
                    chosen,
                    jnp.dot(
                        jnp.concatenate((band * ahead_b, band * beyond_b), axis=1),
                        grads,
                        preferred_element_type=jnp.float32,
                    ),
                    back,
                )
                outer = nt_dot(jnp.where(chosen, own, jnp.zeros_like(own)), mixed)
                tap_sum[group] += outer[:, :size] * prev + outer[:, size:] * here
            out_ref[rows, lanes] = out.astype(bf16)
            grad_ref[rows, lanes] = back.astype(bf16)
        return carried

    lax.fori_loop(0, SPAN // size, block, 0)
    mirror = jnp.where(across + down == size - 1, 1.0, 0.0)
    for group in range(CONV_GROUPS):
        upside = jnp.dot(
            mirror,
            tap_sum[group],
            precision=lax.Precision.HIGHEST,
            preferred_element_type=jnp.float32,
        )
        turned = pltpu.roll(upside, 1, 1, stride=1, stride_axis=0)
        tap_ref[group : group + 1, :] = jnp.sum(turned, axis=0, keepdims=True)


def return_kernel(
    dq, dk, dv, out, back, taps, dq_o, dk_o, dv_o, out_o, back_o, taps_o,
    slots, total, send_sem, recv_sem, zsend_sem, zrecv_sem, tap_send, tap_recv,
):
    z, p = place_in_slice()
    greet(z, p)
    shares = []
    for step in range(1, PLANES):
        copy = pltpu.make_async_remote_copy(
            src_ref=taps,
            dst_ref=slots.at[step - 1],
            send_sem=zsend_sem.at[step - 1],
            recv_sem=zrecv_sem.at[step - 1],
            device_id=device_of(lax.rem(z + step, PLANES), p),
            device_id_type=MESH,
        )
        copy.start()
        shares.append(copy)

    def send(slot, src, dst, width, block):
        mine = dst.at[:, pl.ds(pl.multiple_of(block(p) * width, width), width)]

        def rows(r):
            return src.at[pl.ds(pl.multiple_of(r * ROWS, ROWS), ROWS), :]

        pltpu.make_async_copy(rows(p), mine, recv_sem.at[slot]).start()

        def step(i, carried):
            r = lax.rem(p + i, PLANE)
            pltpu.make_async_remote_copy(
                src_ref=rows(r),
                dst_ref=mine,
                send_sem=send_sem.at[slot],
                recv_sem=recv_sem.at[slot],
                device_id=device_of(z, r),
                device_id_type=MESH,
            ).start()
            return carried

        lax.fori_loop(1, PLANE, step, 0)

    head = lambda r: r
    send(0, out, out_o, CONV_WIDTH, conv_block)
    send(1, back, back_o, CONV_WIDTH, conv_block)
    send(2, dq, dq_o, HEAD_DIM, head)
    send(3, dk, dk_o, HEAD_DIM, head)
    send(4, dv, dv_o, HEAD_DIM, head)
    for copy in shares:
        copy.wait()
    total[...] = taps[...] + slots[0] + slots[1] + slots[2]
    mine = taps_o.at[pl.ds(pl.multiple_of(lax.div(p, 4) * CONV_GROUPS, CONV_GROUPS), CONV_GROUPS), :]
    pltpu.make_async_copy(total, mine, tap_recv).start()

    def tell(i, carried):
        pltpu.make_async_remote_copy(
            src_ref=total,
            dst_ref=mine,
            send_sem=tap_send,
            recv_sem=tap_recv,
            device_id=device_of(z, lax.rem(p + 4 * i, PLANE)),
            device_id_type=MESH,
        ).start()
        return carried

    lax.fori_loop(1, PLANE // 4, tell, 0)
    for slot, (src, dst) in enumerate(
        ((out, out_o), (back, back_o), (dq, dq_o), (dk, dk_o), (dv, dv_o))
    ):
        wait_bytes(dst, recv_sem.at[slot])
        wait_bytes(src.at[pl.ds(0, SPAN - ROWS), :], send_sem.at[slot])
    wait_bytes(taps_o, tap_recv)
    wait_bytes(taps_o.at[pl.ds(0, FILTER_LEN - CONV_GROUPS), :], tap_send)


def hand_back(dq, dk, dv, out, back, taps):
    bf16 = jnp.bfloat16
    any_space = pl.BlockSpec(memory_space=pl.ANY)
    attn = jax.ShapeDtypeStruct((ROWS, PLANE * HEAD_DIM), bf16)
    conv = jax.ShapeDtypeStruct((ROWS, PLANE * CONV_WIDTH), bf16)
    dma = pltpu.SemaphoreType.DMA
    return pl.pallas_call(
        return_kernel,
        out_shape=(
            attn, attn, attn, conv, conv, jax.ShapeDtypeStruct((128, FILTER_LEN), jnp.float32),
        ),
        in_specs=[any_space] * 5 + [pl.BlockSpec(memory_space=pltpu.VMEM)],
        out_specs=(any_space,) * 6,
        scratch_shapes=[
            pltpu.VMEM((PLANES - 1, CONV_GROUPS, FILTER_LEN), jnp.float32),
            pltpu.VMEM((CONV_GROUPS, FILTER_LEN), jnp.float32),
            dma((5,)), dma((5,)), dma((3,)), dma((3,)), dma, dma,
        ],
        compiler_params=pltpu.CompilerParams(collective_id=1, has_side_effects=True),
        name="hand_back",
    )(dq, dk, dv, out, back, taps)


def call_local(kernel, name, out_shape, scratch, flops, *operands):
    vmem = pl.BlockSpec(memory_space=pltpu.VMEM)
    moved = sum(x.size * x.dtype.itemsize for x in operands)
    return pl.pallas_call(
        kernel,
        out_shape=out_shape,
        in_specs=[pl.BlockSpec(memory_space=pltpu.SMEM)] + [vmem] * (len(operands) - 1),
        out_specs=jax.tree.map(lambda _: vmem, out_shape),
        scratch_shapes=scratch,
        compiler_params=pltpu.CompilerParams(vmem_limit_bytes=VMEM_LIMIT),
        cost_estimate=pl.CostEstimate(flops=flops, bytes_accessed=moved, transcendentals=0),
        name=name,
    )(*operands)


def body(
    attn_query, attn_key, attn_value, attn_output, attn_grad_out,
    conv_query, conv_key, conv_value, conv_grad_out, conv_filter, doc_lengths,
):
    f32, bf16 = jnp.float32, jnp.bfloat16
    mixed = (conv_key.astype(f32) * conv_value.astype(f32)).astype(bf16)
    out_grad = (conv_grad_out.astype(f32) * conv_query.astype(f32)).astype(bf16)
    qw, kw, vw, ow, gw, mw, ogw = spread(
        attn_query, attn_key, attn_value, attn_output, attn_grad_out, mixed, out_grad
    )
    shape = jax.ShapeDtypeStruct
    own_stats = call_local(
        stats_kernel, "stats", shape((NEAR, 8, TILE), f32), [], 10**9, doc_lengths, qw, kw, gw, ow
    )
    seq_count = PLANE // 4 * PLANES

    def from_later(block, planes):
        shift = planes * (PLANE // 4)
        return lax.ppermute(
            block, "seq", [(i, (i - shift) % seq_count) for i in range(seq_count)]
        )

    near_stats = from_later(own_stats, 1)
    far_stats = from_later(own_stats[:1], 2)
    _, p = place_in_slice()
    taps = lax.dynamic_slice_in_dim(
        conv_filter, lax.div(p, 4) * CONV_GROUPS, CONV_GROUPS, 0
    ).astype(f32)
    flip = lambda rows: jnp.roll(rows[:, ::-1], 1, axis=1)
    square = (CONV_GROUPS, FILTER_LEN, FILTER_LEN)
    out, back, tap_grad = call_local(
        conv_kernel,
        "conv",
        (
            shape((SPAN, CONV_WIDTH), bf16),
            shape((SPAN, CONV_WIDTH), bf16),
            shape((CONV_GROUPS, FILTER_LEN), f32),
        ),
        [pltpu.VMEM(square, bf16), pltpu.VMEM(square, bf16), pltpu.VMEM(square, f32)],
        4 * 10**9,
        doc_lengths, taps, flip(taps), mw, ogw,
    )
    attn = shape((SPAN, HEAD_DIM), bf16)
    dq, dk, dv = call_local(
        grads_kernel,
        "grads",
        (attn, attn, attn),
        [
            pltpu.VMEM((NEAR + REACH, 8, TILE), f32),
            pltpu.VMEM((SPAN, HEAD_DIM), f32),
            pltpu.VMEM((SPAN, HEAD_DIM), f32),
            pltpu.VMEM((HEAD_DIM, TILE), f32),
        ],
        3 * 10**9,
        doc_lengths, qw, kw, vw, gw, own_stats, near_stats, far_stats,
    )
    dq, dk, dv, out, back, filter_grad = hand_back(dq, dk, dv, out, back, flip(tap_grad))
    back = back.astype(f32)
    return (
        dq,
        dk,
        dv,
        (conv_grad_out.astype(f32) * out.astype(f32)).astype(bf16),
        (back * conv_value.astype(f32)).astype(bf16),
        (back * conv_key.astype(f32)).astype(bf16),
        filter_grad,
    )


def solution(mesh):
    rows = P(("seq", "ch"), None)
    return jax.shard_map(
        body,
        mesh=mesh,
        in_specs=(rows,) * 9 + (P("ch", None), P()),
        out_specs=(rows,) * 6 + (P("ch", None),),
        check_vma=False,
    )
```

time: 1130 us -> 114 us (0.10)
  waiting for transfers between devices: 638 us -> 0.01 us
  local copies, waits for them, and re-layouts: 225 us -> 7.01 us
  starting transfers between devices: 153 us -> 5.85 us
  Pallas kernels: 0 us -> 91.9 us
  matrix products: 70.3 us -> 0 us
  other arithmetic: 24.6 us -> 8 us
  between operations: 14.7 us -> 0.72 us
    psum x1 -> x0, waiting for transfers between devices: 341 us -> none  [body(): grad_filter = lax.psum(tap_grad, 'seq')]
    ppermute x32 -> x2, waiting for transfers between devices: 248 us -> 0.01 us  [from_later(): lax.ppermute(block, 'seq', [(i, (i - shift) % seq_count) for i in range(s...]
    reshape x26 -> x0, local copies, waits for them, and re-layouts: 93.8 us -> none  [the longest x8 33.9 us: band_sums(): skewed = flattened.reshape(group_count, row_count, span_count + 2)]
    pallas_call x0 -> x5, Pallas kernels: none -> 91.9 us  [the longest x1 37.1 us: spread(): pl.pallas_call(spread_kernel, out_shape=(window, window, window, jax.Shap...]
    ppermute x32 -> x2, starting transfers between devices: 97.7 us -> 5.85 us  [from_later(): lax.ppermute(block, 'seq', [(i, (i - shift) % seq_count) for i in range(s...]
    dot_general x85 -> x0, matrix products: 70.3 us -> none  [the longest x11 12.9 us: key_step(): jnp.einsum('thd,rhd->htr', query_heads, key_part, preferred_element_type=...]
    all_to_all x15 -> x0, starting transfers between devices: 55.3 us -> none  [the longest x1 4.88 us: body(): lax.all_to_all(grad_value, 'ch', split_axis=0, concat_axis=1, tiled=True)]
    all_to_all x15 -> x0, waiting for transfers between devices: 47.6 us -> none  [the longest x1 7.88 us: body(): lax.all_to_all(grad_mixer_key, 'ch', split_axis=0, concat_axis=1, tiled=T...]
  transfers between devices with their start and end apart: 48 -> 2, of which waited for: 40 -> 0; matrix products, arithmetic and copies ran while one was open for 28% -> 3% of each run, Pallas kernels for 0% -> 11%
where the time goes in v1:
time: 114 us
  Pallas kernels  91.9 us (81%)
  other arithmetic  8 us (7%)
  local copies, waits for them, and re-layouts  7.01 us (6%)
  starting transfers between devices  5.85 us (5%)
    pallas_call x1, Pallas kernels, spread(): pl.pallas_call(spread_kernel, out_shape=(window, window, window, jax.Shap...  37.1 us
    pallas_call x1, Pallas kernels, hand_back(): pl.pallas_call(return_kernel, out_shape=(attn, attn, attn, conv, conv, ja...  32 us
    pallas_call x3, Pallas kernels, call_local(): pl.pallas_call(kernel, out_shape=out_shape, in_specs=[pl.BlockSpec(memory...  22.9 us
    ppermute x2, starting transfers between devices, from_later(): lax.ppermute(block, 'seq', [(i, (i - shift) % seq_count) for i in range(s...  5.85 us
    unnamed x28, local copies, waits for them, and re-layouts  5.29 us
    convert_element_type x1, other arithmetic, body(): mixed = (conv_key.astype(f32) * conv_value.astype(f32)).astype(bf16)  2.72 us
  transfers between devices with their start and end apart: 2, of which 0 were waited for; matrix products, arithmetic and copies ran while one was open for 3% of the time, Pallas kernels for 11%

profile of v1, /device:TPU:0, one launch (start us, length us, event | category | flops | bytes accessed | tf_op | source)
XLA Modules:
  0.0 113.5 jit_solution(15769835413872478796)
XLA Ops:
  0.6 2.7 %fusion = (bf16[32,8192]{1,0:T(8,128)(2,1)}, bf16[32,8192]{1,0:T(8,128)(2,1)}) fusion(bf16[32,8192]{1,0:T(8,128)(2,1)} %param.18, bf16[32,8192]{1,0:T(8,128)(2,1)} %param.17, bf16[32,8192]{1,0:T(8,128)(2,1)} %param.16, bf16[32,8192]{1,0:T(8,128)(2,1)} %param.19), kind=kLoop, calls=%fused_computation.5 | loop fusion | flops 2097152 | bytes 3145728 | tf_op jit(solution)/shard_map/convert_element_type | solution.py:524
  3.4 37.1 %spread.1 = (bf16[2304,128]{1,0:T(8,128)(2,1)}, bf16[2304,128]{1,0:T(8,128)(2,1)}, bf16[2304,128]{1,0:T(8,128)(2,1)}, bf16[1024,128]{1,0:T(8,128)(2,1)}, bf16[23...) custom-call(bf16[32,4096]{1,0:T(8,128)(2,1)} %q.1, bf16[32,4096]{1,0:T(8,128)(2,1)} %k.1, ...), custom_call_target="tpu_custom_call" | custom-call | tf_op jit(solution)/shard_map/spread/pallas_call | solution.py:144
  40.5 4.4 %stats.1.own_stats = f32[4,8,256]{2,1,0:T(8,128)} custom-call(s32[12]{0:T(128)} %len_ref.5, bf16[2304,128]{1,0:T(8,128)(2,1)} %get-tuple-element.26.qw, bf16[2304,128]{1,0:T(8,128)(2,1)} %get-tuple-element.27.kw, bf16[2304,128]{1,0:T(8,128)(2,1)} %get-tuple-element.29.gw, bf16[1024,128]{1,0:T(8,128)(2,1)} %get-tuple-element.30.ow), custom_call_target="tpu_custom_call" | custom-call | flops 1000000000 | bytes 2031664 | tf_op jit(solution)/shard_map/stats/pallas_call | solution.py:507
  44.9 4.5 %collective-permute-start = (f32[4,8,256]{2,1,0:T(8,128)}, f32[4,8,256]{2,1,0:T(8,128)S(1)}, u32[]{:S(2)}, u32[]{:S(2)}) collective-permute-start(f32[4,8,256]{2,1,0:T(8,128)} %stats.1.own_stats), channel_id=1, source_target_pairs={{0,96},{4,100},{8,104},{12,108},{16,112},{20,116},{24,120},{28,124... | collective-permute-start | bytes 98312 | tf_op jit(solution)/shard_map/ppermute | solution.py:537
  49.4 0.7 slice.32
  50.1 1.3 %collective-permute-start.1 = (f32[1,8,256]{2,1,0:T(8,128)S(1)}, f32[1,8,256]{2,1,0:T(8,128)S(1)}, u32[]{:S(2)}, u32[]{:S(2)}) collective-permute-start(f32[1,8,256]{2,1,0:T(8,128)S(1)} %slice.32), channel_id=1, source_target_pairs={{0,64},{4,68},{8,72},{12,76},{16,80},{20,84},{24,88},{28,92},{32,9... | collective-permute-start | bytes 24584 | tf_op jit(solution)/shard_map/ppermute | solution.py:537
  51.5 0.7 dynamic-slice_convert_fusion.taps
  52.2 0.0 copy-start.7
  52.2 0.1 slice.34
  52.2 0.1 slice.28
  52.3 0.4 copy-done.7
  52.8 0.7 pad_maximum_fusion.back_taps
  53.4 12.0 %conv.1 = (bf16[1024,256]{1,0:T(8,128)(2,1)}, bf16[1024,256]{1,0:T(8,128)(2,1)}, f32[16,128]{1,0:T(8,128)}) custom-call(s32[12]{0:T(128)} %len_ref.5, f32[16,128]{1,0:T(8,128)} %copy-done.7, f32[16,128]{1,0:T(8,128)} %pad_maximum_fusion.back_taps, bf16[1152,256]{1,0:T(8,128)(2,1)} %get-tuple-element.34.mw, bf16[1152,256]{1,0:T(8,128)(2,1)} %get-tuple-element.35.ogw), custom_call_target="tpu_custom_call" | custom-call | flops 4000000000 | bytes 1196080 | tf_op jit(solution)/shard_map/conv/pallas_call | solution.py:507
  65.5 0.8 slice.30
  66.2 0.0 copy-start.9
  66.2 0.1 slice.31
  66.3 0.6 copy-done.9
  66.9 0.7 pad_maximum_fusion.1.taps
  67.6 0.0 collective-permute-done.1.far_stats
  67.6 0.0 copy-start.11
  67.6 0.0 collective-permute-done.near_stats
  67.6 0.0 copy-start.10
  67.6 0.6 copy-done.11
  68.2 0.0 copy-done.10
  68.2 6.4 %grads.1 = (bf16[1024,128]{1,0:T(8,128)(2,1)}, bf16[1024,128]{1,0:T(8,128)(2,1)}, bf16[1024,128]{1,0:T(8,128)(2,1)}) custom-call(s32[12]{0:T(128)} %len_ref.5, bf16[2304,128]{1,0:T(8,128)(2,1)} %get-tuple-element.26.qw, bf16[2304,128]{1,0:T(8,128)(2,1)} %get-tuple-element.27.kw, bf16[2304,128]{1,0:T(8,128)(2,1)} %get-tuple-element.28.vw, ...), custom_call_target="tpu_custom_call" | custom-call | flops 3000000000 | bytes 2433072 | tf_op jit(solution)/shard_map/grads/pallas_call | solution.py:507
  74.6 0.0 copy-start
  74.6 32.0 %hand_back.1 = (bf16[32,4096]{1,0:T(8,128)(2,1)}, bf16[32,4096]{1,0:T(8,128)(2,1)}, bf16[32,4096]{1,0:T(8,128)(2,1)}, bf16[32,8192]{1,0:T(8,128)(2,1)}, bf16[32,8192]{1,0:T(8,128)(2,1)}, /*index=5*/f32[128,128]{1,0:T(8,128)}) custom-call(bf16[1024,128]{1,0:T(8,128)(2,1)} %get-tuple-element.31.dq, bf16[1024,128]{1,0:T(8,128)(2,1)} %get-tuple-element.32.dk, ...), custom_call_target="tpu_custom_call" | custom-call | tf_op jit(solution)/shard_map/hand_back/pallas_call | solution.py:487
  106.6 0.0 copy-done
  106.6 0.0 copy-start.1
  106.6 0.0 copy-start.2
  106.7 0.0 copy-start.3
  106.7 2.1 %fusion.2 = bf16[32,8192]{1,0:T(8,128)(2,1)} fusion(bf16[32,8192]{1,0:T(8,128)(2,1)S(1)} %copy-done, bf16[32,8192]{1,0:T(8,128)(2,1)} %get-tuple-element.42), kind=kLoop, calls=%fused_computation.7 | loop fusion | flops 1048576 | bytes 1572864 | tf_op jit(solution)/shard_map/convert_element_type | solution.py:581
  108.7 0.0 copy-done.1
  108.7 0.0 copy-done.2
  108.7 0.0 copy-done.3
  108.7 0.0 copy-start.6
  108.8 1.2 %fusion.4 = (bf16[32,8192]{1,0:T(8,128)(2,1)}, bf16[32,8192]{1,0:T(8,128)(2,1)}) fusion(bf16[32,8192]{1,0:T(8,128)(2,1)S(1)} %copy-done.2, bf16[32,8192]{1,0:T(8,128)(2,1)S(1)} %copy-done.3, bf16[32,8192]{1,0:T(8,128)(2,1)S(1)} %copy-done.1), kind=kLoop, calls=%fused_computation.9 | loop fusion | flops 1835008 | bytes 2621440 | tf_op jit(solution)/shard_map/convert_element_type | solution.py:583
  109.9 0.0 copy-done.6
  109.9 0.0 copy-start.5
  109.9 0.7 copy.22
  110.6 0.3 copy-done.5
  111.0 0.0 copy-start.4
  111.0 0.7 copy.23
  111.7 0.3 copy-done.4
  112.0 0.0 copy-start.8
  112.0 0.7 copy.24
  112.7 0.2 copy-done.8
  112.9 0.6 copy.25
Async XLA Ops:
  44.9 22.7 %collective-permute-start = (f32[4,8,256]{2,1,0:T(8,128)}, f32[4,8,256]{2,1,0:T(8,128)S(1)}, u32[]{:S(2)}, u32[]{:S(2)}) collective-permute-start(f32[4,8,256]{2,1,0:T(8,128)} %stats.1.own_stats), channel_id=1, source_target_pairs={{0,96},{4,100},{8,104},{12,108},{16,112},{20,116},{24,120},{28,124... | collective-permute-start | bytes 98312 | tf_op jit(solution)/shard_map/ppermute | solution.py:537
  50.1 17.5 %collective-permute-start.1 = (f32[1,8,256]{2,1,0:T(8,128)S(1)}, f32[1,8,256]{2,1,0:T(8,128)S(1)}, u32[]{:S(2)}, u32[]{:S(2)}) collective-permute-start(f32[1,8,256]{2,1,0:T(8,128)S(1)} %slice.32), channel_id=1, source_target_pairs={{0,64},{4,68},{8,72},{12,76},{16,80},{20,84},{24,88},{28,92},{32,9... | collective-permute-start | bytes 24584 | tf_op jit(solution)/shard_map/ppermute | solution.py:537
  52.2 0.6 copy-start.7
  66.2 0.7 copy-start.9
  67.6 0.6 copy-start.11
  67.6 0.6 copy-start.10
  74.6 32.0 %copy-start = (bf16[32,8192]{1,0:T(8,128)(2,1)S(1)}, bf16[32,8192]{1,0:T(8,128)(2,1)}, u32[]{:S(2)}) copy-start(bf16[32,8192]{1,0:T(8,128)(2,1)} %param.19) | copy-start | bytes 1572868
  106.6 2.1 %copy-start.1 = (bf16[32,8192]{1,0:T(8,128)(2,1)S(1)}, bf16[32,8192]{1,0:T(8,128)(2,1)}, u32[]{:S(2)}) copy-start(bf16[32,8192]{1,0:T(8,128)(2,1)} %param.18) | copy-start | bytes 1572868
  106.6 2.1 %copy-start.2 = (bf16[32,8192]{1,0:T(8,128)(2,1)S(1)}, bf16[32,8192]{1,0:T(8,128)(2,1)}, u32[]{:S(2)}) copy-start(bf16[32,8192]{1,0:T(8,128)(2,1)} %param.17) | copy-start | bytes 1572868
  106.7 2.1 %copy-start.3 = (bf16[32,8192]{1,0:T(8,128)(2,1)S(1)}, bf16[32,8192]{1,0:T(8,128)(2,1)}, u32[]{:S(2)}) copy-start(bf16[32,8192]{1,0:T(8,128)(2,1)} %get-tuple-element.43) | copy-start | bytes 1572868
  108.7 1.2 %copy-start.6 = (bf16[32,4096]{1,0:T(8,128)(2,1)S(1)}, bf16[32,4096]{1,0:T(8,128)(2,1)}, u32[]{:S(2)}) copy-start(bf16[32,4096]{1,0:T(8,128)(2,1)} %get-tuple-element.56) | copy-start | bytes 786436
  109.9 1.0 copy-start.5
  111.0 1.0 copy-start.4
  112.0 0.9 copy-start.8

commit v2 on v1

v2 whole, which is shorter than its diff:
```python
import math

import jax
import jax.numpy as jnp
from jax import lax
from jax.experimental import pallas as pl
from jax.experimental.pallas import tpu as pltpu
from jax.sharding import PartitionSpec as P

MESH = pl.DeviceIdType.MESH
HEAD_DIM = 128
FILTER_LEN = 128
DOCS = 12
PLANE = 32
PLANES = 4
ROWS = 32
SPAN = PLANE * ROWS
TILE = 256
NEAR = SPAN // TILE
REACH = 5
WINDOW = SPAN + REACH * TILE
CONV_WIDTH = 256
CONV_GROUPS = 16
LOG2_SCALE = math.log2(math.e) / math.sqrt(HEAD_DIM)
SCALE = 1.0 / math.sqrt(HEAD_DIM)
NEG_FILL = -1e30
VMEM_LIMIT = 60 * 1024 * 1024


def place_in_slice():
    me = lax.axis_index("seq") * 4 + lax.axis_index("ch")
    return lax.div(me, PLANE), lax.rem(me, PLANE)


def device_of(z, p):
    return (z * (PLANE // 4) + lax.div(p, 4), lax.rem(p, 4))


def conv_block(p):
    return lax.rem(p, 4) * (PLANE // 4) + lax.div(p, 4)


def greet(z, p):
    barrier = pltpu.get_barrier_semaphore()

    def hello(k, carried):
        pl.semaphore_signal(
            barrier, inc=1, device_id=device_of(z, lax.rem(p + k, PLANE)), device_id_type=MESH
        )
        return carried

    lax.fori_loop(1, PLANE, hello, 0)
    for step in range(1, PLANES):
        pl.semaphore_signal(
            barrier, inc=1, device_id=device_of(lax.rem(z + step, PLANES), p), device_id_type=MESH
        )
    pl.semaphore_wait(barrier, PLANE - 1 + PLANES - 1)


def wait_bytes(ref, sem):
    pltpu.make_async_copy(ref, ref, sem).wait()


def doc_ends(len_ref):
    ends = []
    total = jnp.int32(0)
    for d in range(DOCS):
        total = total + len_ref[d]
        ends.append(total)
    return ends


def doc_start(ends, pos):
    start = jnp.zeros_like(pos)
    for end in ends:
        start = jnp.maximum(start, jnp.where(end <= pos, end, 0))
    return start


def doc_stop(ends, pos):
    stop = jnp.full_like(pos, ends[-1])
    for end in ends:
        stop = jnp.minimum(stop, jnp.where(end > pos, end, ends[-1]))
    return stop


def nt_dot(a, b):
    return lax.dot_general(a, b, (((1,), (1,)), ((), ())), preferred_element_type=jnp.float32)


def tile_rows(ref, i):
    return ref[pl.ds(pl.multiple_of(i * TILE, TILE), TILE), :]


def row_positions(base):
    return base + lax.broadcasted_iota(jnp.int32, (1, TILE), 1)


def first_tile(ends, z, q_base):
    start = doc_start(ends, q_base)
    return lax.div(start - (z * SPAN - REACH * TILE), TILE)


def seen_before(z, kb, starts):
    k_pos = z * SPAN - REACH * TILE + kb * TILE + lax.broadcasted_iota(jnp.int32, (TILE, TILE), 0)
    return k_pos >= starts


def seen_diagonal(z, kb, starts):
    below = lax.broadcasted_iota(jnp.int32, (TILE, TILE), 0) <= lax.broadcasted_iota(
        jnp.int32, (TILE, TILE), 1
    )
    return seen_before(z, kb, starts) & below


def gather_kernel(
    len_ref, q, k, v, o, g, cq, ck, cv, cg, filt,
    kv_out, qg_out, stats_out, back_out, taps_out,
    kv_in, qg_in, o_in, conv_in, pair, delta_in, delta, kv, qg, conv, result, circ, back_circ,
    tap_sum, taps, stats, running,
    load_sem, send_sem, recv_sem, zsend_sem, zrecv_sem, out_sem,
):
    z, p = place_in_slice()
    ends = doc_ends(len_ref)
    f32, bf16 = jnp.float32, jnp.bfloat16
    loads = []
    for i, (src, dst) in enumerate(
        (
            (k, kv_in.at[0]), (v, kv_in.at[1]), (q, qg_in.at[0]), (g, qg_in.at[1]), (o, o_in),
            (ck, conv_in.at[0]), (cv, conv_in.at[1]), (cg, conv_in.at[2]), (cq, conv_in.at[3]),
        )
    ):
        copy = pltpu.make_async_copy(src, dst, load_sem.at[i])
        copy.start()
        loads.append(copy)
    greet(z, p)

    def send(slot, take, give):
        pltpu.make_async_copy(take(p), give, recv_sem.at[slot]).start()

        def step(i, carried):
            r = lax.rem(p + i, PLANE)
            pltpu.make_async_remote_copy(
                src_ref=take(r),
                dst_ref=give,
                send_sem=send_sem.at[slot],
                recv_sem=recv_sem.at[slot],
                device_id=device_of(z, r),
                device_id_type=MESH,
            ).start()
            return carried

        lax.fori_loop(1, PLANE, step, 0)

    hops = {}

    def hop(slot, src, dst, step):
        copy = pltpu.make_async_remote_copy(
            src_ref=src,
            dst_ref=dst,
            send_sem=zsend_sem.at[slot],
            recv_sem=zrecv_sem.at[slot],
            device_id=device_of(lax.rem(z + step, PLANES), p),
            device_id_type=MESH,
        )
        copy.start()
        hops[slot] = copy

    def head_columns(ref):
        return lambda r: ref.at[:, :, pl.ds(pl.multiple_of(r * HEAD_DIM, HEAD_DIM), HEAD_DIM)]

    def conv_columns(ref, half):
        return lambda r: ref.at[
            :, :, pl.ds(pl.multiple_of(conv_block(r) * CONV_WIDTH + half * 128, 128), 128)
        ]

    def my_rows(base):
        return pl.ds(pl.multiple_of(base + p * ROWS, ROWS), ROWS)

    back = REACH * TILE
    size = FILTER_LEN
    loads[0].wait()
    loads[1].wait()
    send(0, head_columns(kv_in), kv.at[:, my_rows(back), :])
    loads[2].wait()
    loads[3].wait()
    send(1, head_columns(qg_in), qg.at[:, my_rows(0), :])
    for i in (5, 6, 7, 8):
        loads[i].wait()

    def products(i, carried):
        lanes = pl.ds(pl.multiple_of(i * 512, 512), 512)
        pair[0, :, lanes] = (
            conv_in[0, :, lanes].astype(f32) * conv_in[1, :, lanes].astype(f32)
        ).astype(bf16)
        pair[1, :, lanes] = (
            conv_in[2, :, lanes].astype(f32) * conv_in[3, :, lanes].astype(f32)
        ).astype(bf16)
        return carried

    lax.fori_loop(0, PLANE * CONV_WIDTH // 512, products, 0)
    loads[4].wait()

    def deltas(h, carried):
        lanes = pl.ds(pl.multiple_of(h * HEAD_DIM, HEAD_DIM), HEAD_DIM)
        terms = qg_in[1, :, lanes].astype(f32) * o_in[:, lanes].astype(f32)
        padded = jnp.concatenate((terms, jnp.zeros((HEAD_DIM - ROWS, HEAD_DIM), f32)), axis=0)
        delta_in[h] = jnp.sum(padded.T, axis=0, keepdims=True)
        return carried

    lax.fori_loop(0, PLANE, deltas, 0)
    send(2, conv_columns(pair, 0), conv.at[0, :, my_rows(size), :])
    send(3, lambda r: delta_in.at[r], delta.at[p])
    send(4, conv_columns(pair, 1), conv.at[1, :, my_rows(size), :])

    down = lax.broadcasted_iota(jnp.int32, (size, size), 0)
    across = lax.broadcasted_iota(jnp.int32, (size, size), 1)
    mirror = jnp.where(lax.rem(across + down, size) == 0, 1.0, 0.0)
    own_taps = filt[
        pl.ds(pl.multiple_of(lax.div(p, 4) * CONV_GROUPS, CONV_GROUPS), CONV_GROUPS), :
    ]
    flipped = jnp.dot(own_taps, mirror.astype(bf16), preferred_element_type=f32)
    own_taps = own_taps.astype(f32)
    for group in range(CONV_GROUPS):
        for src, dst in ((own_taps, circ), (flipped, back_circ)):
            row = jnp.broadcast_to(src[group : group + 1, :], (size, size))
            dst[group] = pltpu.roll(row, 0, 1, stride=1, stride_axis=0).astype(bf16)
    tap_sum[...] = jnp.zeros_like(tap_sum)
    stats[0:NEAR] = jnp.zeros((NEAR, 8, TILE), f32)

    wait_bytes(kv.at[:, pl.ds(back, SPAN), :], recv_sem.at[0])
    hop(0, kv.at[:, pl.ds(back, SPAN), :], kv.at[:, pl.ds(TILE, SPAN), :], 1)
    hop(1, kv.at[:, pl.ds(SPAN + back - TILE, TILE), :], kv.at[:, pl.ds(0, TILE), :], 2)
    wait_bytes(qg.at[:, pl.ds(0, SPAN), :], recv_sem.at[1])
    hop(2, qg.at[:, pl.ds(0, SPAN), :], qg.at[:, pl.ds(SPAN, SPAN), :], 3)
    hop(3, qg.at[:, pl.ds(0, TILE), :], qg.at[:, pl.ds(2 * SPAN, TILE), :], 2)

    def scores(qi, kb, seen):
        starts = doc_start(ends, row_positions(z * SPAN + qi * TILE))
        s = nt_dot(tile_rows(kv.at[0], kb), tile_rows(qg.at[0], qi)) * LOG2_SCALE
        return jnp.where(seen(z, kb, starts), s, NEG_FILL)

    def extend(qi, kb, state):
        top, total = state
        s = scores(qi, kb, seen_before)
        new_top = jnp.maximum(top, jnp.max(s, axis=0, keepdims=True))
        total = total * jnp.exp2(top - new_top) + jnp.sum(
            jnp.exp2(s - new_top), axis=0, keepdims=True
        )
        return new_top, total

    def own_tiles(qi, carried):
        s = scores(qi, qi + REACH, seen_diagonal)
        top = jnp.max(s, axis=0, keepdims=True)
        total = jnp.sum(jnp.exp2(s - top), axis=0, keepdims=True)
        top, total = lax.fori_loop(
            REACH, REACH + qi, lambda kb, state: extend(qi, kb, state), (top, total)
        )
        running[qi, 0:1, :] = top
        running[qi, 1:2, :] = total
        return carried

    def earlier_tiles(qi, carried):
        top, total = lax.fori_loop(
            qi,
            REACH,
            lambda kb, state: extend(qi, kb, state),
            (running[qi, 0:1, :], running[qi, 1:2, :]),
        )
        stats[qi, 0:1, :] = top + jnp.log2(total)
        for side in range(2):
            row = jnp.zeros((1, HEAD_DIM), f32)
            for part in range(4):
                row = row + pltpu.roll(delta[qi * 8 + side * 4 + part], part * ROWS, 1)
            stats[qi, 1:2, side * HEAD_DIM : (side + 1) * HEAD_DIM] = row
        return carried

    def conv_rows(half, kind, start, count):
        return conv.at[half, kind, pl.ds(start, count), :]

    def halo(half):
        wait_bytes(conv.at[half, :, pl.ds(size, SPAN), :], recv_sem.at[2 + 2 * half])
        hop(4 + half, conv_rows(half, 0, SPAN, size), conv_rows(half, 0, 0, size), 1)
        hop(6 + half, conv_rows(half, 1, size, size), conv_rows(half, 1, SPAN + size, size), 3)

    group_of_lane = lax.div(across, 16)

    def conv_tile(half, tb):
        base = z * SPAN + tb * size
        positions = base + lax.broadcasted_iota(jnp.int32, (1, size), 1)

        def as_column(row):
            return jnp.broadcast_to(row.astype(f32), (size, size)).T.astype(jnp.int32)

        start = as_column(doc_start(ends, positions))
        stop = as_column(doc_stop(ends, positions))
        prev = jnp.where((across > down) & (base - size + across >= start), 1.0, 0.0)
        here = jnp.where((across <= down) & (base + across >= start), 1.0, 0.0)
        ahead = jnp.where((across >= down) & (base + across < stop), 1.0, 0.0)
        beyond = jnp.where((across < down) & (base + size + across < stop), 1.0, 0.0)
        prev_b, here_b = prev.astype(bf16), here.astype(bf16)
        ahead_b, beyond_b = ahead.astype(bf16), beyond.astype(bf16)
        rows = pl.ds(pl.multiple_of(tb * size, size), size)
        here_rows = pl.ds(pl.multiple_of(tb * size + size, size), size)
        mixed = conv[half, 0, pl.ds(pl.multiple_of(tb * size, size), 2 * size), :]
        grads = conv[half, 1, pl.ds(pl.multiple_of(tb * size + size, size), 2 * size), :]
        own = conv[half, 1, here_rows, :]
        out = jnp.zeros((size, size), f32)
        inner = jnp.zeros((size, size), f32)
        for member in range(8):
            group = half * 8 + member
            chosen = group_of_lane == member
            band = back_circ[group]
            out = jnp.where(
                chosen,
                jnp.dot(
                    jnp.concatenate((band * prev_b, band * here_b), axis=1),
                    mixed,
                    preferred_element_type=f32,
                ),
                out,
            )
            band = circ[group]
            inner = jnp.where(
                chosen,
                jnp.dot(
                    jnp.concatenate((band * ahead_b, band * beyond_b), axis=1),
                    grads,
                    preferred_element_type=f32,
                ),
                inner,
            )
            outer = nt_dot(jnp.where(chosen, own, jnp.zeros_like(own)), mixed)
            tap_sum[group] += outer[:, :size] * prev + outer[:, size:] * here
        result[half, 0, rows, :] = out.astype(bf16)
        result[half, 1, rows, :] = inner.astype(bf16)

    def conv_back(half, tb):
        columns = pl.ds(pl.multiple_of(conv_block(p) * CONV_WIDTH + half * 128, 128), 128)
        mine = back_out.at[:, :, columns]

        def one(i, carried):
            r = tb * 4 + i
            rows = result.at[half, :, pl.ds(pl.multiple_of(r * ROWS, ROWS), ROWS), :]

            @pl.when(r == p)
            def _():
                pltpu.make_async_copy(rows, mine, recv_sem.at[5]).start()

            @pl.when(r != p)
            def _():
                pltpu.make_async_remote_copy(
                    src_ref=rows,
                    dst_ref=mine,
                    send_sem=send_sem.at[5],
                    recv_sem=recv_sem.at[5],
                    device_id=device_of(z, r),
                    device_id_type=MESH,
                ).start()

            return carried

        lax.fori_loop(0, 4, one, 0)

    def conv_half(half):
        turn = lax.div(p, 4)

        def inner_tile(i, carried):
            tb = 1 + lax.rem(i + turn, 6)
            conv_tile(half, tb)
            conv_back(half, tb)
            return carried

        def edge_tile(i, carried):
            tb = 7 * lax.rem(i + turn, 2)
            conv_tile(half, tb)
            conv_back(half, tb)
            return carried

        lax.fori_loop(0, 6, inner_tile, 0)
        hops[4 + half].wait()
        hops[6 + half].wait()
        lax.fori_loop(0, 2, edge_tile, 0)

    lax.fori_loop(0, NEAR, own_tiles, 0)
    wait_bytes(delta, recv_sem.at[3])
    halo(0)
    conv_half(0)
    halo(1)
    hops[0].wait()
    hops[1].wait()
    kv_copy = pltpu.make_async_copy(kv, kv_out, out_sem.at[0])
    kv_copy.start()
    lax.fori_loop(0, NEAR, earlier_tiles, 0)
    conv_half(1)
    hop(8, stats.at[pl.ds(0, NEAR)], stats.at[pl.ds(NEAR, NEAR)], 3)
    hop(9, stats.at[pl.ds(0, 1)], stats.at[pl.ds(2 * NEAR, 1)], 2)
    hops[2].wait()
    hops[3].wait()
    qg_copy = pltpu.make_async_copy(qg, qg_out, out_sem.at[1])
    qg_copy.start()
    upside_down = jnp.where(across + down == size - 1, 1.0, 0.0)
    for group in range(CONV_GROUPS):
        upside = jnp.dot(
            upside_down, tap_sum[group], precision=lax.Precision.HIGHEST, preferred_element_type=f32
        )
        turned = pltpu.roll(upside, 1, 1, stride=1, stride_axis=0)
        taps[0, group : group + 1, :] = jnp.sum(turned, axis=0, keepdims=True)
    hops[8].wait()
    hops[9].wait()
    stats_copy = pltpu.make_async_copy(stats, stats_out, out_sem.at[2])
    stats_copy.start()
    for step in range(1, PLANES):
        hop(9 + step, taps.at[0], taps.at[step], step)
    for step in range(1, PLANES):
        hops[9 + step].wait()
    taps_copy = pltpu.make_async_copy(taps, taps_out, out_sem.at[3])
    taps_copy.start()
    most = PLANE - 1
    wait_bytes(kv.at[:, pl.ds(0, most * ROWS), :], send_sem.at[0])
    wait_bytes(qg.at[:, pl.ds(0, most * ROWS), :], send_sem.at[1])
    wait_bytes(conv.at[0, :, pl.ds(0, most * ROWS), :], send_sem.at[2])
    wait_bytes(delta.at[pl.ds(0, most)], send_sem.at[3])
    wait_bytes(conv.at[1, :, pl.ds(0, most * ROWS), :], send_sem.at[4])
    wait_bytes(back_out.at[:, :, pl.ds(0, most * CONV_WIDTH)], send_sem.at[5])
    wait_bytes(back_out, recv_sem.at[5])
    for copy in (kv_copy, qg_copy, stats_copy, taps_copy):
        copy.wait()


def gather(doc_lengths, q, k, v, o, g, cq, ck, cv, cg, filt):
    f32, bf16 = jnp.float32, jnp.bfloat16
    any_space = pl.BlockSpec(memory_space=pl.ANY)
    shape = jax.ShapeDtypeStruct
    vmem, dma = pltpu.VMEM, pltpu.SemaphoreType.DMA
    square = (CONV_GROUPS, FILTER_LEN, FILTER_LEN)
    features, channels = PLANE * HEAD_DIM, PLANE * CONV_WIDTH
    return pl.pallas_call(
        gather_kernel,
        out_shape=(
            shape((2, WINDOW, HEAD_DIM), bf16),
            shape((2, WINDOW, HEAD_DIM), bf16),
            shape((NEAR + REACH, 8, TILE), f32),
            shape((2, ROWS, channels), bf16),
            shape((PLANES, CONV_GROUPS, FILTER_LEN), f32),
        ),
        in_specs=[pl.BlockSpec(memory_space=pltpu.SMEM)]
        + [any_space] * 9
        + [pl.BlockSpec(memory_space=pltpu.VMEM)],
        out_specs=(any_space,) * 5,
        scratch_shapes=[
            vmem((2, ROWS, features), bf16),
            vmem((2, ROWS, features), bf16),
            vmem((ROWS, features), bf16),
            vmem((4, ROWS, channels), bf16),
            vmem((2, ROWS, channels), bf16),
            vmem((PLANE, 1, HEAD_DIM), f32),
            vmem((PLANE, 1, HEAD_DIM), f32),
            vmem((2, WINDOW, HEAD_DIM), bf16),
            vmem((2, WINDOW, HEAD_DIM), bf16),
            vmem((2, 2, SPAN + 2 * FILTER_LEN, 128), bf16),
            vmem((2, 2, SPAN, 128), bf16),
            vmem(square, bf16),
            vmem(square, bf16),
            vmem(square, f32),
            vmem((PLANES, CONV_GROUPS, FILTER_LEN), f32),
            vmem((NEAR + REACH, 8, TILE), f32),
            vmem((NEAR, 8, TILE), f32),
            dma((9,)), dma((6,)), dma((6,)), dma((13,)), dma((13,)), dma((4,)),
        ],
        compiler_params=pltpu.CompilerParams(
            collective_id=0, has_side_effects=True, vmem_limit_bytes=VMEM_LIMIT
        ),
        name="gather",
    )(doc_lengths, q, k, v, o, g, cq, ck, cv, cg, filt)


def grads_kernel(
    len_ref, kv, qg, stats, taps, back, cg, cv, ck,
    grads_out, gcq, gck, gcv, taps_out,
    dk_sum, dv_sum, dq_sum, conv_in, conv_res, load_sem, store_sem,
):
    z, _ = place_in_slice()
    ends = doc_ends(len_ref)
    f32, bf16 = jnp.float32, jnp.bfloat16
    kw, vw, qw, gw = kv.at[0], kv.at[1], qg.at[0], qg.at[1]
    loads = [
        pltpu.make_async_copy(src, dst, load_sem.at[i])
        for i, (src, dst) in enumerate(
            (
                (back.at[0], conv_in.at[0]), (back.at[1], conv_in.at[1]),
                (cg, conv_in.at[2]), (cv, conv_in.at[3]), (ck, conv_in.at[4]),
            )
        )
    ]
    for copy in loads:
        copy.start()
    dk_sum[...] = jnp.zeros_like(dk_sum)
    dv_sum[...] = jnp.zeros_like(dv_sum)
    size = FILTER_LEN
    down = lax.broadcasted_iota(jnp.int32, (size, size), 0)
    across = lax.broadcasted_iota(jnp.int32, (size, size), 1)
    mirror = jnp.where(lax.rem(across + down, size) == 0, 1.0, 0.0)
    taps_out[...] = jnp.dot(
        (taps[0] + taps[1]) + (taps[2] + taps[3]),
        mirror,
        precision=lax.Precision.HIGHEST,
        preferred_element_type=f32,
    )

    def pair(qi, kb, starts, seen, for_query, for_key):
        query = tile_rows(qw, qi)
        grad = tile_rows(gw, qi)
        key = tile_rows(kw, kb)
        s = nt_dot(key, query) * LOG2_SCALE - stats[qi, 0:1, :]
        probs = jnp.where(seen(z, kb, starts), jnp.exp2(s), 0.0)
        grad_scores = probs * (nt_dot(tile_rows(vw, kb), grad) - stats[qi, 1:2, :])
        grad_scores = grad_scores.astype(jnp.bfloat16)
        if for_key:
            rows = pl.ds(pl.multiple_of((kb - REACH) * TILE, TILE), TILE)
            dv_sum[rows, :] += jnp.dot(
                probs.astype(jnp.bfloat16), grad, preferred_element_type=jnp.float32
            )
            dk_sum[rows, :] += jnp.dot(grad_scores, query, preferred_element_type=jnp.float32)
        if for_query:
            dq_sum[...] += lax.dot_general(
                key, grad_scores, (((0,), (0,)), ((), ())), preferred_element_type=jnp.float32
            )

    def own_tile(qi, carried):
        q_base = z * SPAN + qi * TILE
        starts = doc_start(ends, row_positions(q_base))
        first = first_tile(ends, z, q_base)
        dq_sum[...] = jnp.zeros_like(dq_sum)

        def before(kb, inner):
            pair(qi, kb, starts, seen_before, True, False)
            return inner

        def within(kb, inner):
            pair(qi, kb, starts, seen_before, True, True)
            return inner

        lax.fori_loop(first, REACH, before, 0)
        lax.fori_loop(jnp.maximum(first, REACH), REACH + qi, within, 0)
        pair(qi, REACH + qi, starts, seen_diagonal, True, True)
        rows = pl.ds(pl.multiple_of(qi * TILE, TILE), TILE)
        grads_out[0, rows, :] = (dq_sum[...].T * SCALE).astype(jnp.bfloat16)
        return carried

    lax.fori_loop(0, NEAR, own_tile, 0)
    for copy in loads:
        copy.wait()

    def gates(i, carried):
        lanes = pl.ds(pl.multiple_of(i * 512, 512), 512)
        inner = conv_in[1, :, lanes].astype(f32)
        pieces = (
            (0, conv_in[0, :, lanes].astype(f32), 2), (1, inner, 3), (2, inner, 4),
        )
        for slot, left, right in pieces:
            conv_res[slot, :, lanes] = (left * conv_in[right, :, lanes].astype(f32)).astype(bf16)
        return carried

    lax.fori_loop(0, PLANE * CONV_WIDTH // 512, gates, 0)
    stores = [
        pltpu.make_async_copy(conv_res.at[i], dst, store_sem.at[i])
        for i, dst in enumerate((gcq, gck, gcv))
    ]
    for copy in stores:
        copy.start()

    def later_tile(qi, carried):
        q_base = z * SPAN + qi * TILE
        starts = doc_start(ends, row_positions(q_base))

        def after(kb, inner):
            pair(qi, kb, starts, seen_before, False, True)
            return inner

        first = jnp.maximum(first_tile(ends, z, q_base), REACH)
        lax.fori_loop(first, REACH + NEAR, after, 0)
        return carried

    lax.fori_loop(NEAR, NEAR + REACH, later_tile, 0)
    grads_out[1] = (dk_sum[...] * SCALE).astype(jnp.bfloat16)
    grads_out[2] = dv_sum[...].astype(jnp.bfloat16)
    for copy in stores:
        copy.wait()


def local_grads(doc_lengths, kv, qg, stats, taps, back, cg, cv, ck):
    f32, bf16 = jnp.float32, jnp.bfloat16
    any_space = pl.BlockSpec(memory_space=pl.ANY)
    vmem_space = pl.BlockSpec(memory_space=pltpu.VMEM)
    shape = jax.ShapeDtypeStruct
    rows = shape(cg.shape, bf16)
    return pl.pallas_call(
        grads_kernel,
        out_shape=(
            shape((3, SPAN, HEAD_DIM), bf16),
            rows,
            rows,
            rows,
            shape((CONV_GROUPS, FILTER_LEN), f32),
        ),
        in_specs=[pl.BlockSpec(memory_space=pltpu.SMEM)] + [vmem_space] * 4 + [any_space] * 4,
        out_specs=(vmem_space, any_space, any_space, any_space, vmem_space),
        scratch_shapes=[
            pltpu.VMEM((SPAN, HEAD_DIM), f32),
            pltpu.VMEM((SPAN, HEAD_DIM), f32),
            pltpu.VMEM((HEAD_DIM, TILE), f32),
            pltpu.VMEM((5,) + cg.shape, bf16),
            pltpu.VMEM((3,) + cg.shape, bf16),
            pltpu.SemaphoreType.DMA((5,)),
            pltpu.SemaphoreType.DMA((3,)),
        ],
        compiler_params=pltpu.CompilerParams(vmem_limit_bytes=VMEM_LIMIT),
        name="grads",
    )(doc_lengths, kv, qg, stats, taps, back, cg, cv, ck)


def return_kernel(grads, taps, grads_o, taps_o, send_sem, recv_sem, tap_send, tap_recv):
    z, p = place_in_slice()
    greet(z, p)
    mine = grads_o.at[:, :, pl.ds(pl.multiple_of(p * HEAD_DIM, HEAD_DIM), HEAD_DIM)]

    def rows(r):
        return grads.at[:, pl.ds(pl.multiple_of(r * ROWS, ROWS), ROWS), :]

    pltpu.make_async_copy(rows(p), mine, recv_sem).start()
    taps_at = pl.ds(pl.multiple_of(lax.div(p, 4) * CONV_GROUPS, CONV_GROUPS), CONV_GROUPS)
    pltpu.make_async_copy(taps, taps_o.at[taps_at, :], tap_recv).start()

    def tell(i, carried):
        pltpu.make_async_remote_copy(
            src_ref=taps,
            dst_ref=taps_o.at[taps_at, :],
            send_sem=tap_send,
            recv_sem=tap_recv,
            device_id=device_of(z, lax.rem(p + 4 * i, PLANE)),
            device_id_type=MESH,
        ).start()
        return carried

    def step(i, carried):
        r = lax.rem(p + i, PLANE)
        pltpu.make_async_remote_copy(
            src_ref=rows(r),
            dst_ref=mine,
            send_sem=send_sem,
            recv_sem=recv_sem,
            device_id=device_of(z, r),
            device_id_type=MESH,
        ).start()
        return carried

    lax.fori_loop(1, PLANE, step, 0)
    lax.fori_loop(1, PLANE // 4, tell, 0)
    wait_bytes(grads_o, recv_sem)
    wait_bytes(grads.at[:, pl.ds(0, SPAN - ROWS), :], send_sem)
    wait_bytes(taps_o, tap_recv)
    wait_bytes(taps_o.at[pl.ds(0, FILTER_LEN - CONV_GROUPS), :], tap_send)


def hand_back(grads, taps):
    any_space = pl.BlockSpec(memory_space=pl.ANY)
    dma = pltpu.SemaphoreType.DMA
    return pl.pallas_call(
        return_kernel,
        out_shape=(
            jax.ShapeDtypeStruct((3, ROWS, PLANE * HEAD_DIM), jnp.bfloat16),
            jax.ShapeDtypeStruct((128, FILTER_LEN), jnp.float32),
        ),
        in_specs=[any_space] * 2,
        out_specs=(any_space,) * 2,
        scratch_shapes=[dma, dma, dma, dma],
        compiler_params=pltpu.CompilerParams(collective_id=1, has_side_effects=True),
        name="hand_back",
    )(grads, taps)


def finish_kernel(grads, taps, dq, dk, dv, taps_out):
    dq[...] = grads[0]
    dk[...] = grads[1]
    dv[...] = grads[2]
    taps_out[...] = taps[...]


def finish(grads, taps):
    vmem_space = pl.BlockSpec(memory_space=pltpu.VMEM)
    rows = jax.ShapeDtypeStruct(grads.shape[1:], grads.dtype)
    return pl.pallas_call(
        finish_kernel,
        out_shape=(rows, rows, rows, jax.ShapeDtypeStruct(taps.shape, taps.dtype)),
        in_specs=[vmem_space] * 2,
        out_specs=(vmem_space,) * 4,
        name="finish",
    )(grads, taps)


def body(
    attn_query, attn_key, attn_value, attn_output, attn_grad_out,
    conv_query, conv_key, conv_value, conv_grad_out, conv_filter, doc_lengths,
):
    kv, qg, stats, back, taps = gather(
        doc_lengths, attn_query, attn_key, attn_value, attn_output, attn_grad_out,
        conv_query, conv_key, conv_value, conv_grad_out, conv_filter,
    )
    grads, gcq, gck, gcv, taps = local_grads(
        doc_lengths, kv, qg, stats, taps, back, conv_grad_out, conv_value, conv_key
    )
    dq, dk, dv, filter_grad = finish(*hand_back(grads, taps))
    return dq, dk, dv, gcq, gck, gcv, filter_grad


def solution(mesh):
    rows = P(("seq", "ch"), None)
    return jax.shard_map(
        body,
        mesh=mesh,
        in_specs=(rows,) * 9 + (P("ch", None), P()),
        out_specs=(rows,) * 6 + (P("ch", None),),
        check_vma=False,
    )
```

time: 114 us -> 89.1 us (0.78)
  other arithmetic: 8 us -> 0 us
  local copies, waits for them, and re-layouts: 7.01 us -> 0 us
  starting transfers between devices: 5.85 us -> 0 us
  Pallas kernels: 91.9 us -> 88.4 us
    convert_element_type x4 -> x0, other arithmetic: 6.65 us -> none  [the longest x1 2.72 us: body(): mixed = (conv_key.astype(f32) * conv_value.astype(f32)).astype(bf16)]
    ppermute x2 -> x0, starting transfers between devices: 5.85 us -> none  [from_later(): lax.ppermute(block, 'seq', [(i, (i - shift) % seq_count) for i in range(s...]
    unnamed x28 -> x0, local copies, waits for them, and re-layouts: 5.29 us -> none
    pallas_call x5 -> x4, Pallas kernels: 91.9 us -> 88.4 us  [the longest x1 58.4 us: gather(): pl.pallas_call(gather_kernel, out_shape=(shape((2, WINDOW, HEAD_DIM), bf1...]
    slice x5 -> x0, local copies, waits for them, and re-layouts: 1.72 us -> none  [the longest x4 0.99 us: body(): flip = lambda rows: jnp.roll(rows[:, ::-1], 1, axis=1)]
    concatenate x2 -> x0, other arithmetic: 1.34 us -> none  [body(): flip = lambda rows: jnp.roll(rows[:, ::-1], 1, axis=1)]
  transfers between devices with their start and end apart: 2 -> 0, of which waited for: 0 -> 0; matrix products, arithmetic and copies ran while one was open for 3% -> 0% of each run, Pallas kernels for 11% -> 0%
where the time goes in v2:
time: 89.1 us; the launch traced here: 89 us
  Pallas kernels  88.4 us (99%)
    pallas_call x1, Pallas kernels, gather(): pl.pallas_call(gather_kernel, out_shape=(shape((2, WINDOW, HEAD_DIM), bf1...  58.4 us
    pallas_call x1, Pallas kernels, hand_back(): pl.pallas_call(return_kernel, out_shape=(jax.ShapeDtypeStruct((3, ROWS, P...  19.4 us
    pallas_call x1, Pallas kernels, local_grads(): pl.pallas_call(grads_kernel, out_shape=(shape((3, SPAN, HEAD_DIM), bf16),...  8.64 us
    pallas_call x1, Pallas kernels, finish(): pl.pallas_call(finish_kernel, out_shape=(rows, rows, rows, jax.ShapeDtype...  2.04 us

profile of v2, /device:TPU:0, one launch (start us, length us, event | category | flops | bytes accessed | tf_op | source)
XLA Modules:
  0.0 89.0 jit_solution(16154111413612663733)
XLA Ops:
  0.6 58.4 %gather.1 = (bf16[2,2304,128]{2,1,0:T(8,128)(2,1)}, bf16[2,2304,128]{2,1,0:T(8,128)(2,1)}, f32[9,8,256]{2,1,0:T(8,128)}, bf16[2,32,8192]{2,1,0:T(8,128)(2,1)}, f32[4,16,128]{2,1,0:T(8,128)}) custom-call(s32[12]{0:T(128)} %len_ref.3, bf16[32,4096]{1,0:T(8,128)(2,1)} %q.1, bf16[32,4096]{1,0:T(8,128)(2,1)} %k.1, bf16[32,4096]{1,0:T(8,128)(2,1)} %v.1, ...), custom_call_target="tpu_custom_call" | custom-call | tf_op jit(solution)/shard_map/gather/pallas_call | solution.py:438
  59.0 8.6 %grads.1 = (bf16[3,1024,128]{2,1,0:T(8,128)(2,1)}, bf16[32,8192]{1,0:T(8,128)(2,1)}, bf16[32,8192]{1,0:T(8,128)(2,1)}, bf16[32,8192]{1,0:T(8,128)(2,1)}, f32[16,128]{1,0:T(8,128)}) custom-call(s32[12]{0:T(128)} %len_ref.3, bf16[2,2304,128]{2,1,0:T(8,128)(2,1)} %get-tuple-element.23.kv, bf16[2,2304,128]{2,1,0:T(8,128)(2,1)} %get-tuple-element.24.qg, ...), custom_call_target="tpu_custom_call" | custom-call | tf_op jit(solution)/shard_map/grads/pallas_call | solution.py:598
  67.6 19.4 %hand_back.1 = (bf16[3,32,4096]{2,1,0:T(8,128)(2,1)}, f32[128,128]{1,0:T(8,128)}) custom-call(bf16[3,1024,128]{2,1,0:T(8,128)(2,1)} %get-tuple-element.28.grads, f32[16,128]{1,0:T(8,128)} %get-tuple-element.29.taps), custom_call_target="tpu_custom_call" | custom-call | tf_op jit(solution)/shard_map/hand_back/pallas_call | solution.py:669
  87.0 2.0 %finish.1 = (bf16[32,4096]{1,0:T(8,128)(2,1)}, bf16[32,4096]{1,0:T(8,128)(2,1)}, bf16[32,4096]{1,0:T(8,128)(2,1)}, f32[128,128]{1,0:T(8,128)}) custom-call(bf16[3,32,4096]{2,1,0:T(8,128)(2,1)} %get-tuple-element.30.grads, f32[128,128]{1,0:T(8,128)} %get-tuple-element.31.taps), custom_call_target="tpu_custom_call" | custom-call | tf_op jit(solution)/shard_map/finish/pallas_call | solution.py:693

commit v3 on v2

--- a/solution.py
+++ b/solution.py
@@ -40,6 +40,15 @@
     return lax.rem(p, 4) * (PLANE // 4) + lax.div(p, 4)
 
 
+def partner(p, i):
+    turn, member = lax.div(i, 16), lax.rem(i, 16)
+    across = lax.rem(member, 4)
+    down = lax.rem(lax.div(member, 4) + 3 * member, 4)
+    x = lax.rem(lax.rem(lax.div(p, 2), 4) + across, 4)
+    y = lax.rem(lax.div(p, 8) + down, 4)
+    return y * 8 + x * 2 + lax.rem(p + turn, 2)
+
+
 def greet(z, p):
     barrier = pltpu.get_barrier_semaphore()
 
@@ -96,11 +105,6 @@
     return base + lax.broadcasted_iota(jnp.int32, (1, TILE), 1)
 
 
-def first_tile(ends, z, q_base):
-    start = doc_start(ends, q_base)
-    return lax.div(start - (z * SPAN - REACH * TILE), TILE)
-
-
 def seen_before(z, kb, starts):
     k_pos = z * SPAN - REACH * TILE + kb * TILE + lax.broadcasted_iota(jnp.int32, (TILE, TILE), 0)
     return k_pos >= starts
@@ -113,12 +117,12 @@
     return seen_before(z, kb, starts) & below
 
 
-def gather_kernel(
+def exchange_kernel(
     len_ref, q, k, v, o, g, cq, ck, cv, cg, filt,
-    kv_out, qg_out, stats_out, back_out, taps_out,
+    grads_out, back_out, taps_out,
     kv_in, qg_in, o_in, conv_in, pair, delta_in, delta, kv, qg, conv, result, circ, back_circ,
-    tap_sum, taps, stats, running,
-    load_sem, send_sem, recv_sem, zsend_sem, zrecv_sem, out_sem,
+    tap_sum, folded, taps, stats, running, saved, tops, dk_sum, dv_sum, dq_sum, grads, tap_total,
+    load_sem, send_sem, recv_sem, zsend_sem, zrecv_sem,
 ):
     z, p = place_in_slice()
     ends = doc_ends(len_ref)
@@ -139,7 +143,7 @@
         pltpu.make_async_copy(take(p), give, recv_sem.at[slot]).start()
 
         def step(i, carried):
-            r = lax.rem(p + i, PLANE)
+            r = partner(p, i)
             pltpu.make_async_remote_copy(
                 src_ref=take(r),
                 dst_ref=give,
@@ -240,19 +244,24 @@
         s = nt_dot(tile_rows(kv.at[0], kb), tile_rows(qg.at[0], qi)) * LOG2_SCALE
         return jnp.where(seen(z, kb, starts), s, NEG_FILL)
 
+    def keep(qi, kb, s, top):
+        slot = qi * REACH + kb
+        weights = jnp.exp2(s - top)
+        saved[slot] = weights
+        tops[slot, 0:1, :] = top
+        return jnp.sum(weights, axis=0, keepdims=True)
+
     def extend(qi, kb, state):
         top, total = state
         s = scores(qi, kb, seen_before)
         new_top = jnp.maximum(top, jnp.max(s, axis=0, keepdims=True))
-        total = total * jnp.exp2(top - new_top) + jnp.sum(
-            jnp.exp2(s - new_top), axis=0, keepdims=True
-        )
+        total = total * jnp.exp2(top - new_top) + keep(qi, kb, s, new_top)
         return new_top, total
 
     def own_tiles(qi, carried):
         s = scores(qi, qi + REACH, seen_diagonal)
         top = jnp.max(s, axis=0, keepdims=True)
-        total = jnp.sum(jnp.exp2(s - top), axis=0, keepdims=True)
+        total = keep(qi, qi + REACH, s, top)
         top, total = lax.fori_loop(
             REACH, REACH + qi, lambda kb, state: extend(qi, kb, state), (top, total)
         )
@@ -382,6 +391,87 @@
         hops[6 + half].wait()
         lax.fori_loop(0, 2, edge_tile, 0)
 
+    def add_pair(qi, kb, probs, for_query, for_key):
+        query = tile_rows(qg.at[0], qi)
+        grad = tile_rows(qg.at[1], qi)
+        grad_probs = nt_dot(tile_rows(kv.at[1], kb), grad)
+        grad_scores = (probs * (grad_probs - stats[qi, 1:2, :])).astype(bf16)
+        if for_key:
+            rows = pl.ds(pl.multiple_of((kb - REACH) * TILE, TILE), TILE)
+            dv_sum[rows, :] += jnp.dot(probs.astype(bf16), grad, preferred_element_type=f32)
+            dk_sum[rows, :] += jnp.dot(grad_scores, query, preferred_element_type=f32)
+        if for_query:
+            dq_sum[...] += lax.dot_general(
+                tile_rows(kv.at[0], kb),
+                grad_scores,
+                (((0,), (0,)), ((), ())),
+                preferred_element_type=f32,
+            )
+
+    head_lanes = pl.ds(pl.multiple_of(p * HEAD_DIM, HEAD_DIM), HEAD_DIM)
+
+    def query_back(qi):
+        mine = grads_out.at[0, :, head_lanes]
+
+        def one(i, carried):
+            r = qi * 8 + lax.rem(i + p, 8)
+            rows = grads.at[0, pl.ds(pl.multiple_of(r * ROWS, ROWS), ROWS), :]
+
+            @pl.when(r == p)
+            def _():
+                pltpu.make_async_copy(rows, mine, recv_sem.at[6]).start()
+
+            @pl.when(r != p)
+            def _():
+                pltpu.make_async_remote_copy(
+                    src_ref=rows,
+                    dst_ref=mine,
+                    send_sem=send_sem.at[6],
+                    recv_sem=recv_sem.at[6],
+                    device_id=device_of(z, r),
+                    device_id_type=MESH,
+                ).start()
+
+            return carried
+
+        lax.fori_loop(0, 8, one, 0)
+
+    def own_grads(i, carried):
+        qi = lax.rem(i + lax.div(p, 8), NEAR)
+        dq_sum[...] = jnp.zeros_like(dq_sum)
+
+        def probs_of(kb):
+            slot = qi * REACH + kb
+            return saved[slot] * jnp.exp2(tops[slot, 0:1, :] - stats[qi, 0:1, :])
+
+        def before(kb, inner):
+            add_pair(qi, kb, probs_of(kb), True, False)
+            return inner
+
+        def within(kb, inner):
+            add_pair(qi, kb, probs_of(kb), True, True)
+            return inner
+
+        lax.fori_loop(qi, REACH, before, 0)
+        lax.fori_loop(REACH, REACH + qi + 1, within, 0)
+        rows = pl.ds(pl.multiple_of(qi * TILE, TILE), TILE)
+        grads[0, rows, :] = (dq_sum[...].T * SCALE).astype(bf16)
+        query_back(qi)
+        return carried
+
+    def later_grads(qi, carried):
+        starts = doc_start(ends, row_positions(z * SPAN + qi * TILE))
+
+        def after(kb, inner):
+            s = nt_dot(tile_rows(kv.at[0], kb), tile_rows(qg.at[0], qi)) * LOG2_SCALE
+            s = s - stats[qi, 0:1, :]
+            probs = jnp.where(seen_before(z, kb, starts), jnp.exp2(s), 0.0)
+            add_pair(qi, kb, probs, False, True)
+            return inner
+
+        lax.fori_loop(jnp.maximum(qi, REACH), REACH + NEAR, after, 0)
+        return carried
+
     lax.fori_loop(0, NEAR, own_tiles, 0)
     wait_bytes(delta, recv_sem.at[3])
     halo(0)
@@ -389,33 +479,66 @@
     halo(1)
     hops[0].wait()
     hops[1].wait()
-    kv_copy = pltpu.make_async_copy(kv, kv_out, out_sem.at[0])
-    kv_copy.start()
     lax.fori_loop(0, NEAR, earlier_tiles, 0)
-    conv_half(1)
     hop(8, stats.at[pl.ds(0, NEAR)], stats.at[pl.ds(NEAR, NEAR)], 3)
     hop(9, stats.at[pl.ds(0, 1)], stats.at[pl.ds(2 * NEAR, 1)], 2)
+    conv_half(1)
+
+    def fold(group, carried):
+        total = jnp.zeros((8, size), f32)
+        for step in range(size // 8):
+            rows = tap_sum[group, 8 * step : 8 * step + 8, :]
+            total = total + pltpu.roll(rows, (size - 8 * step) % size, 1)
+        folded[group] = total
+        return carried
+
+    lax.fori_loop(0, CONV_GROUPS, fold, 0)
+    total = folded[:, 0, :]
+    for step in range(1, 8):
+        total = total + pltpu.roll(folded[:, step, :], size - step, 1)
+    taps[0] = total
+    dk_sum[...] = jnp.zeros_like(dk_sum)
+    dv_sum[...] = jnp.zeros_like(dv_sum)
+    for step in range(1, PLANES):
+        hop(9 + step, taps.at[0], taps.at[step], step)
+    lax.fori_loop(0, NEAR, own_grads, 0)
+    for step in range(1, PLANES):
+        hops[9 + step].wait()
+    tap_total[...] = jnp.dot(
+        (taps[0] + taps[1]) + (taps[2] + taps[3]),
+        mirror,
+        precision=lax.Precision.HIGHEST,
+        preferred_element_type=f32,
+    )
+    hops[8].wait()
+    hops[9].wait()
     hops[2].wait()
     hops[3].wait()
-    qg_copy = pltpu.make_async_copy(qg, qg_out, out_sem.at[1])
-    qg_copy.start()
-    upside_down = jnp.where(across + down == size - 1, 1.0, 0.0)
-    for group in range(CONV_GROUPS):
-        upside = jnp.dot(
-            upside_down, tap_sum[group], precision=lax.Precision.HIGHEST, preferred_element_type=f32
-        )
-        turned = pltpu.roll(upside, 1, 1, stride=1, stride_axis=0)
-        taps[0, group : group + 1, :] = jnp.sum(turned, axis=0, keepdims=True)
-    hops[8].wait()
-    hops[9].wait()
-    stats_copy = pltpu.make_async_copy(stats, stats_out, out_sem.at[2])
-    stats_copy.start()
-    for step in range(1, PLANES):
-        hop(9 + step, taps.at[0], taps.at[step], step)
-    for step in range(1, PLANES):
-        hops[9 + step].wait()
-    taps_copy = pltpu.make_async_copy(taps, taps_out, out_sem.at[3])
-    taps_copy.start()
+    lax.fori_loop(NEAR, NEAR + REACH, later_grads, 0)
+    grads[1] = (dk_sum[...] * SCALE).astype(bf16)
+    grads[2] = dv_sum[...].astype(bf16)
+    send(
+        7,
+        lambda r: grads.at[pl.ds(1, 2), pl.ds(pl.multiple_of(r * ROWS, ROWS), ROWS), :],
+        grads_out.at[pl.ds(1, 2), :, head_lanes],
+    )
+    tap_rows = taps_out.at[
+        pl.ds(pl.multiple_of(lax.div(p, 4) * CONV_GROUPS, CONV_GROUPS), CONV_GROUPS), :
+    ]
+    pltpu.make_async_copy(tap_total, tap_rows, recv_sem.at[8]).start()
+
+    def tell(i, carried):
+        pltpu.make_async_remote_copy(
+            src_ref=tap_total,
+            dst_ref=tap_rows,
+            send_sem=send_sem.at[8],
+            recv_sem=recv_sem.at[8],
+            device_id=device_of(z, lax.rem(p + 4 * i, PLANE)),
+            device_id_type=MESH,
+        ).start()
+        return carried
+
+    lax.fori_loop(1, PLANE // 4, tell, 0)
     most = PLANE - 1
     wait_bytes(kv.at[:, pl.ds(0, most * ROWS), :], send_sem.at[0])
     wait_bytes(qg.at[:, pl.ds(0, most * ROWS), :], send_sem.at[1])
@@ -424,11 +547,15 @@
     wait_bytes(conv.at[1, :, pl.ds(0, most * ROWS), :], send_sem.at[4])
     wait_bytes(back_out.at[:, :, pl.ds(0, most * CONV_WIDTH)], send_sem.at[5])
     wait_bytes(back_out, recv_sem.at[5])
-    for copy in (kv_copy, qg_copy, stats_copy, taps_copy):
-        copy.wait()
-
-
-def gather(doc_lengths, q, k, v, o, g, cq, ck, cv, cg, filt):
+    wait_bytes(grads.at[0, pl.ds(0, most * ROWS), :], send_sem.at[6])
+    wait_bytes(grads_out.at[0], recv_sem.at[6])
+    wait_bytes(grads.at[pl.ds(1, 2), pl.ds(0, most * ROWS), :], send_sem.at[7])
+    wait_bytes(grads_out.at[pl.ds(1, 2)], recv_sem.at[7])
+    wait_bytes(taps_out.at[pl.ds(0, FILTER_LEN - CONV_GROUPS), :], send_sem.at[8])
+    wait_bytes(taps_out, recv_sem.at[8])
+
+
+def exchange(doc_lengths, q, k, v, o, g, cq, ck, cv, cg, filt):
     f32, bf16 = jnp.float32, jnp.bfloat16
     any_space = pl.BlockSpec(memory_space=pl.ANY)
     shape = jax.ShapeDtypeStruct
@@ -436,18 +563,16 @@
     square = (CONV_GROUPS, FILTER_LEN, FILTER_LEN)
     features, channels = PLANE * HEAD_DIM, PLANE * CONV_WIDTH
     return pl.pallas_call(
-        gather_kernel,
+        exchange_kernel,
         out_shape=(
-            shape((2, WINDOW, HEAD_DIM), bf16),
-            shape((2, WINDOW, HEAD_DIM), bf16),
-            shape((NEAR + REACH, 8, TILE), f32),
+            shape((3, ROWS, features), bf16),
             shape((2, ROWS, channels), bf16),
-            shape((PLANES, CONV_GROUPS, FILTER_LEN), f32),
+            shape((FILTER_LEN, FILTER_LEN), f32),
         ),
         in_specs=[pl.BlockSpec(memory_space=pltpu.SMEM)]
         + [any_space] * 9
         + [pl.BlockSpec(memory_space=pltpu.VMEM)],
-        out_specs=(any_space,) * 5,
+        out_specs=(any_space,) * 3,
         scratch_shapes=[
             vmem((2, ROWS, features), bf16),
             vmem((2, ROWS, features), bf16),
@@ -463,255 +588,72 @@
             vmem(square, bf16),
             vmem(square, bf16),
             vmem(square, f32),
+            vmem((CONV_GROUPS, 8, FILTER_LEN), f32),
             vmem((PLANES, CONV_GROUPS, FILTER_LEN), f32),
             vmem((NEAR + REACH, 8, TILE), f32),
             vmem((NEAR, 8, TILE), f32),
-            dma((9,)), dma((6,)), dma((6,)), dma((13,)), dma((13,)), dma((4,)),
+            vmem((NEAR * (REACH + 1), TILE, TILE), f32),
+            vmem((NEAR * (REACH + 1), 8, TILE), f32),
+            vmem((SPAN, HEAD_DIM), f32),
+            vmem((SPAN, HEAD_DIM), f32),
+            vmem((HEAD_DIM, TILE), f32),
+            vmem((3, SPAN, HEAD_DIM), bf16),
+            vmem((CONV_GROUPS, FILTER_LEN), f32),
+            dma((9,)), dma((9,)), dma((9,)), dma((13,)), dma((13,)),
         ],
         compiler_params=pltpu.CompilerParams(
             collective_id=0, has_side_effects=True, vmem_limit_bytes=VMEM_LIMIT
         ),
-        name="gather",
+        name="exchange",
     )(doc_lengths, q, k, v, o, g, cq, ck, cv, cg, filt)
 
 
-def grads_kernel(
-    len_ref, kv, qg, stats, taps, back, cg, cv, ck,
-    grads_out, gcq, gck, gcv, taps_out,
-    dk_sum, dv_sum, dq_sum, conv_in, conv_res, load_sem, store_sem,
-):
-    z, _ = place_in_slice()
-    ends = doc_ends(len_ref)
+def finish_kernel(grads, taps, back, cg, cv, ck, dq, dk, dv, gcq, gck, gcv, taps_out):
     f32, bf16 = jnp.float32, jnp.bfloat16
-    kw, vw, qw, gw = kv.at[0], kv.at[1], qg.at[0], qg.at[1]
-    loads = [
-        pltpu.make_async_copy(src, dst, load_sem.at[i])
-        for i, (src, dst) in enumerate(
-            (
-                (back.at[0], conv_in.at[0]), (back.at[1], conv_in.at[1]),
-                (cg, conv_in.at[2]), (cv, conv_in.at[3]), (ck, conv_in.at[4]),
-            )
-        )
-    ]
-    for copy in loads:
-        copy.start()
-    dk_sum[...] = jnp.zeros_like(dk_sum)
-    dv_sum[...] = jnp.zeros_like(dv_sum)
-    size = FILTER_LEN
-    down = lax.broadcasted_iota(jnp.int32, (size, size), 0)
-    across = lax.broadcasted_iota(jnp.int32, (size, size), 1)
-    mirror = jnp.where(lax.rem(across + down, size) == 0, 1.0, 0.0)
-    taps_out[...] = jnp.dot(
-        (taps[0] + taps[1]) + (taps[2] + taps[3]),
-        mirror,
-        precision=lax.Precision.HIGHEST,
-        preferred_element_type=f32,
-    )
-
-    def pair(qi, kb, starts, seen, for_query, for_key):
-        query = tile_rows(qw, qi)
-        grad = tile_rows(gw, qi)
-        key = tile_rows(kw, kb)
-        s = nt_dot(key, query) * LOG2_SCALE - stats[qi, 0:1, :]
-        probs = jnp.where(seen(z, kb, starts), jnp.exp2(s), 0.0)
-        grad_scores = probs * (nt_dot(tile_rows(vw, kb), grad) - stats[qi, 1:2, :])
-        grad_scores = grad_scores.astype(jnp.bfloat16)
-        if for_key:
-            rows = pl.ds(pl.multiple_of((kb - REACH) * TILE, TILE), TILE)
-            dv_sum[rows, :] += jnp.dot(
-                probs.astype(jnp.bfloat16), grad, preferred_element_type=jnp.float32
-            )
-            dk_sum[rows, :] += jnp.dot(grad_scores, query, preferred_element_type=jnp.float32)
-        if for_query:
-            dq_sum[...] += lax.dot_general(
-                key, grad_scores, (((0,), (0,)), ((), ())), preferred_element_type=jnp.float32
-            )
-
-    def own_tile(qi, carried):
-        q_base = z * SPAN + qi * TILE
-        starts = doc_start(ends, row_positions(q_base))
-        first = first_tile(ends, z, q_base)
-        dq_sum[...] = jnp.zeros_like(dq_sum)
-
-        def before(kb, inner):
-            pair(qi, kb, starts, seen_before, True, False)
-            return inner
-
-        def within(kb, inner):
-            pair(qi, kb, starts, seen_before, True, True)
-            return inner
-
-        lax.fori_loop(first, REACH, before, 0)
-        lax.fori_loop(jnp.maximum(first, REACH), REACH + qi, within, 0)
-        pair(qi, REACH + qi, starts, seen_diagonal, True, True)
-        rows = pl.ds(pl.multiple_of(qi * TILE, TILE), TILE)
-        grads_out[0, rows, :] = (dq_sum[...].T * SCALE).astype(jnp.bfloat16)
-        return carried
-
-    lax.fori_loop(0, NEAR, own_tile, 0)
-    for copy in loads:
-        copy.wait()
-
-    def gates(i, carried):
-        lanes = pl.ds(pl.multiple_of(i * 512, 512), 512)
-        inner = conv_in[1, :, lanes].astype(f32)
-        pieces = (
-            (0, conv_in[0, :, lanes].astype(f32), 2), (1, inner, 3), (2, inner, 4),
-        )
-        for slot, left, right in pieces:
-            conv_res[slot, :, lanes] = (left * conv_in[right, :, lanes].astype(f32)).astype(bf16)
-        return carried
-
-    lax.fori_loop(0, PLANE * CONV_WIDTH // 512, gates, 0)
-    stores = [
-        pltpu.make_async_copy(conv_res.at[i], dst, store_sem.at[i])
-        for i, dst in enumerate((gcq, gck, gcv))
-    ]
-    for copy in stores:
-        copy.start()
-
-    def later_tile(qi, carried):
-        q_base = z * SPAN + qi * TILE
-        starts = doc_start(ends, row_positions(q_base))
-
-        def after(kb, inner):
-            pair(qi, kb, starts, seen_before, False, True)
-            return inner
-
-        first = jnp.maximum(first_tile(ends, z, q_base), REACH)
-        lax.fori_loop(first, REACH + NEAR, after, 0)
-        return carried
-
-    lax.fori_loop(NEAR, NEAR + REACH, later_tile, 0)
-    grads_out[1] = (dk_sum[...] * SCALE).astype(jnp.bfloat16)
-    grads_out[2] = dv_sum[...].astype(jnp.bfloat16)
-    for copy in stores:
-        copy.wait()
-
-
-def local_grads(doc_lengths, kv, qg, stats, taps, back, cg, cv, ck):
-    f32, bf16 = jnp.float32, jnp.bfloat16
-    any_space = pl.BlockSpec(memory_space=pl.ANY)
-    vmem_space = pl.BlockSpec(memory_space=pltpu.VMEM)
-    shape = jax.ShapeDtypeStruct
-    rows = shape(cg.shape, bf16)
-    return pl.pallas_call(
-        grads_kernel,
-        out_shape=(
-            shape((3, SPAN, HEAD_DIM), bf16),
-            rows,
-            rows,
-            rows,
-            shape((CONV_GROUPS, FILTER_LEN), f32),
-        ),
-        in_specs=[pl.BlockSpec(memory_space=pltpu.SMEM)] + [vmem_space] * 4 + [any_space] * 4,
-        out_specs=(vmem_space, any_space, any_space, any_space, vmem_space),
-        scratch_shapes=[
-            pltpu.VMEM((SPAN, HEAD_DIM), f32),
-            pltpu.VMEM((SPAN, HEAD_DIM), f32),
-            pltpu.VMEM((HEAD_DIM, TILE), f32),
-            pltpu.VMEM((5,) + cg.shape, bf16),
-            pltpu.VMEM((3,) + cg.shape, bf16),
-            pltpu.SemaphoreType.DMA((5,)),
-            pltpu.SemaphoreType.DMA((3,)),
-        ],
-        compiler_params=pltpu.CompilerParams(vmem_limit_bytes=VMEM_LIMIT),
-        name="grads",
-    )(doc_lengths, kv, qg, stats, taps, back, cg, cv, ck)
-
-
-def return_kernel(grads, taps, grads_o, taps_o, send_sem, recv_sem, tap_send, tap_recv):
-    z, p = place_in_slice()
-    greet(z, p)
-    mine = grads_o.at[:, :, pl.ds(pl.multiple_of(p * HEAD_DIM, HEAD_DIM), HEAD_DIM)]
-
-    def rows(r):
-        return grads.at[:, pl.ds(pl.multiple_of(r * ROWS, ROWS), ROWS), :]
-
-    pltpu.make_async_copy(rows(p), mine, recv_sem).start()
-    taps_at = pl.ds(pl.multiple_of(lax.div(p, 4) * CONV_GROUPS, CONV_GROUPS), CONV_GROUPS)
-    pltpu.make_async_copy(taps, taps_o.at[taps_at, :], tap_recv).start()
-
-    def tell(i, carried):
-        pltpu.make_async_remote_copy(
-            src_ref=taps,
-            dst_ref=taps_o.at[taps_at, :],
-            send_sem=tap_send,
-            recv_sem=tap_recv,
-            device_id=device_of(z, lax.rem(p + 4 * i, PLANE)),
-            device_id_type=MESH,
-        ).start()
-        return carried
-
-    def step(i, carried):
-        r = lax.rem(p + i, PLANE)
-        pltpu.make_async_remote_copy(
-            src_ref=rows(r),
-            dst_ref=mine,
-            send_sem=send_sem,
-            recv_sem=recv_sem,
-            device_id=device_of(z, r),
-            device_id_type=MESH,
-        ).start()
-        return carried
-
-    lax.fori_loop(1, PLANE, step, 0)
-    lax.fori_loop(1, PLANE // 4, tell, 0)
-    wait_bytes(grads_o, recv_sem)
-    wait_bytes(grads.at[:, pl.ds(0, SPAN - ROWS), :], send_sem)
-    wait_bytes(taps_o, tap_recv)
-    wait_bytes(taps_o.at[pl.ds(0, FILTER_LEN - CONV_GROUPS), :], tap_send)
-
-
-def hand_back(grads, taps):
-    any_space = pl.BlockSpec(memory_space=pl.ANY)
-    dma = pltpu.SemaphoreType.DMA
-    return pl.pallas_call(
-        return_kernel,
-        out_shape=(
-            jax.ShapeDtypeStruct((3, ROWS, PLANE * HEAD_DIM), jnp.bfloat16),
-            jax.ShapeDtypeStruct((128, FILTER_LEN), jnp.float32),
-        ),
-        in_specs=[any_space] * 2,
-        out_specs=(any_space,) * 2,
-        scratch_shapes=[dma, dma, dma, dma],
-        compiler_params=pltpu.CompilerParams(collective_id=1, has_side_effects=True),
-        name="hand_back",
-    )(grads, taps)
-
-
-def finish_kernel(grads, taps, dq, dk, dv, taps_out):
     dq[...] = grads[0]
     dk[...] = grads[1]
     dv[...] = grads[2]
     taps_out[...] = taps[...]
-
-
-def finish(grads, taps):
-    vmem_space = pl.BlockSpec(memory_space=pltpu.VMEM)
-    rows = jax.ShapeDtypeStruct(grads.shape[1:], grads.dtype)
+    gcq[...] = (cg[...].astype(f32) * back[0].astype(f32)).astype(bf16)
+    inner = back[1].astype(f32)
+    gck[...] = (inner * cv[...].astype(f32)).astype(bf16)
+    gcv[...] = (inner * ck[...].astype(f32)).astype(bf16)
+
+
+FINISH_STEPS = 4
+
+
+def finish(grads, taps, back, cg, cv, ck):
+    features, channels = grads.shape[2], cg.shape[1]
+
+    def rows(width):
+        return pl.BlockSpec((ROWS, width // FINISH_STEPS), lambda i: (0, i))
+
+    def stack(count, width):
+        return pl.BlockSpec((count, ROWS, width // FINISH_STEPS), lambda i: (0, 0, i))
+
+    taps_spec = pl.BlockSpec((FILTER_LEN // FINISH_STEPS, FILTER_LEN), lambda i: (i, 0))
+    attn = jax.ShapeDtypeStruct(grads.shape[1:], grads.dtype)
+    conv = jax.ShapeDtypeStruct(cg.shape, cg.dtype)
     return pl.pallas_call(
         finish_kernel,
-        out_shape=(rows, rows, rows, jax.ShapeDtypeStruct(taps.shape, taps.dtype)),
-        in_specs=[vmem_space] * 2,
-        out_specs=(vmem_space,) * 4,
+        grid=(FINISH_STEPS,),
+        out_shape=(attn,) * 3 + (conv,) * 3 + (jax.ShapeDtypeStruct(taps.shape, taps.dtype),),
+        in_specs=[stack(3, features), taps_spec, stack(2, channels)] + [rows(channels)] * 3,
+        out_specs=(rows(features),) * 3 + (rows(channels),) * 3 + (taps_spec,),
         name="finish",
-    )(grads, taps)
+    )(grads, taps, back, cg, cv, ck)
 
 
 def body(
     attn_query, attn_key, attn_value, attn_output, attn_grad_out,
     conv_query, conv_key, conv_value, conv_grad_out, conv_filter, doc_lengths,
 ):
-    kv, qg, stats, back, taps = gather(
+    grads, back, taps = exchange(
         doc_lengths, attn_query, attn_key, attn_value, attn_output, attn_grad_out,
         conv_query, conv_key, conv_value, conv_grad_out, conv_filter,
     )
-    grads, gcq, gck, gcv, taps = local_grads(
-        doc_lengths, kv, qg, stats, taps, back, conv_grad_out, conv_value, conv_key
-    )
-    dq, dk, dv, filter_grad = finish(*hand_back(grads, taps))
-    return dq, dk, dv, gcq, gck, gcv, filter_grad
+    return finish(grads, taps, back, conv_grad_out, conv_value, conv_key)
 
 
 def solution(mesh):

time: 89.1 us -> 84 us (0.943); the launches traced: 89 us -> 82.7 us
  Pallas kernels: 88.4 us -> 82.1 us
    pallas_call x4 -> x2, Pallas kernels: 88.4 us -> 82.1 us  [the longest x1 77.9 us: exchange(): pl.pallas_call(exchange_kernel, out_shape=(shape((3, ROWS, features), bf1...]
where the time goes in v3:
time: 84 us; the launch traced here: 82.7 us
  Pallas kernels  82.1 us (98%)
    pallas_call x1, Pallas kernels, exchange(): pl.pallas_call(exchange_kernel, out_shape=(shape((3, ROWS, features), bf1...  77.9 us
    pallas_call x1, Pallas kernels, finish(): pl.pallas_call(finish_kernel, grid=(FINISH_STEPS,), out_shape=(attn,) * 3...  4.14 us

profile of v3, /device:TPU:0, one launch (start us, length us, event | category | flops | bytes accessed | tf_op | source)
XLA Modules:
  0.0 82.7 jit_solution(3756899435074543414)
XLA Ops:
  0.6 77.9 %exchange.1 = (bf16[3,32,4096]{2,1,0:T(8,128)(2,1)}, bf16[2,32,8192]{2,1,0:T(8,128)(2,1)}, f32[128,128]{1,0:T(8,128)}) custom-call(s32[12]{0:T(128)} %len_ref.1, bf16[32,4096]{1,0:T(8,128)(2,1)} %q.1, bf16[32,4096]{1,0:T(8,128)(2,1)} %k.1, bf16[32,4096]{1,0:T(8,128)(2,1)} %v.1, bf16[32,4096]{1,0:T(8,128)(2,1)} %o.1, bf16[32,4096]{1,0:T(8,128)(2,1)} %g.1, ...), custom_call_target="tpu_custom_call" | custom-call | tf_op jit(solution)/shard_map/exchange/pallas_call | solution.py:565
  78.6 4.1 %finish.1 = (bf16[32,4096]{1,0:T(8,128)(2,1)}, bf16[32,4096]{1,0:T(8,128)(2,1)}, bf16[32,4096]{1,0:T(8,128)(2,1)}, bf16[32,8192]{1,0:T(8,128)(2,1)}, bf16[32,819...) custom-call(bf16[3,32,4096]{2,1,0:T(8,128)(2,1)} %get-tuple-element.10.grads, ...), custom_call_target="tpu_custom_call" | custom-call | tf_op jit(solution)/shard_map/finish/pallas_call | solution.py:638

commit v4 on v3

--- a/solution.py
+++ b/solution.py
@@ -170,8 +170,8 @@
         copy.start()
         hops[slot] = copy
 
-    def head_columns(ref):
-        return lambda r: ref.at[:, :, pl.ds(pl.multiple_of(r * HEAD_DIM, HEAD_DIM), HEAD_DIM)]
+    def head_columns(ref, kind):
+        return lambda r: ref.at[kind, :, pl.ds(pl.multiple_of(r * HEAD_DIM, HEAD_DIM), HEAD_DIM)]
 
     def conv_columns(ref, half):
         return lambda r: ref.at[
@@ -184,11 +184,9 @@
     back = REACH * TILE
     size = FILTER_LEN
     loads[0].wait()
-    loads[1].wait()
-    send(0, head_columns(kv_in), kv.at[:, my_rows(back), :])
+    send(0, head_columns(kv_in, 0), kv.at[0, my_rows(back), :])
     loads[2].wait()
-    loads[3].wait()
-    send(1, head_columns(qg_in), qg.at[:, my_rows(0), :])
+    send(1, head_columns(qg_in, 0), qg.at[0, my_rows(0), :])
     for i in (5, 6, 7, 8):
         loads[i].wait()
 
@@ -203,7 +201,8 @@
         return carried
 
     lax.fori_loop(0, PLANE * CONV_WIDTH // 512, products, 0)
-    loads[4].wait()
+    for i in (1, 3, 4):
+        loads[i].wait()
 
     def deltas(h, carried):
         lanes = pl.ds(pl.multiple_of(h * HEAD_DIM, HEAD_DIM), HEAD_DIM)
@@ -213,9 +212,9 @@
         return carried
 
     lax.fori_loop(0, PLANE, deltas, 0)
-    send(2, conv_columns(pair, 0), conv.at[0, :, my_rows(size), :])
+    send(9, head_columns(kv_in, 1), kv.at[1, my_rows(back), :])
+    send(10, head_columns(qg_in, 1), qg.at[1, my_rows(0), :])
     send(3, lambda r: delta_in.at[r], delta.at[p])
-    send(4, conv_columns(pair, 1), conv.at[1, :, my_rows(size), :])
 
     down = lax.broadcasted_iota(jnp.int32, (size, size), 0)
     across = lax.broadcasted_iota(jnp.int32, (size, size), 1)
@@ -232,12 +231,13 @@
     tap_sum[...] = jnp.zeros_like(tap_sum)
     stats[0:NEAR] = jnp.zeros((NEAR, 8, TILE), f32)
 
-    wait_bytes(kv.at[:, pl.ds(back, SPAN), :], recv_sem.at[0])
-    hop(0, kv.at[:, pl.ds(back, SPAN), :], kv.at[:, pl.ds(TILE, SPAN), :], 1)
-    hop(1, kv.at[:, pl.ds(SPAN + back - TILE, TILE), :], kv.at[:, pl.ds(0, TILE), :], 2)
-    wait_bytes(qg.at[:, pl.ds(0, SPAN), :], recv_sem.at[1])
-    hop(2, qg.at[:, pl.ds(0, SPAN), :], qg.at[:, pl.ds(SPAN, SPAN), :], 3)
-    hop(3, qg.at[:, pl.ds(0, TILE), :], qg.at[:, pl.ds(2 * SPAN, TILE), :], 2)
+    def key_hops(kind, near, far):
+        hop(near, kv.at[kind, pl.ds(back, SPAN), :], kv.at[kind, pl.ds(TILE, SPAN), :], 1)
+        hop(far, kv.at[kind, pl.ds(SPAN + back - TILE, TILE), :], kv.at[kind, pl.ds(0, TILE), :], 2)
+
+    def query_hops(kind, near, far):
+        hop(near, qg.at[kind, pl.ds(0, SPAN), :], qg.at[kind, pl.ds(SPAN, SPAN), :], 3)
+        hop(far, qg.at[kind, pl.ds(0, TILE), :], qg.at[kind, pl.ds(2 * SPAN, TILE), :], 2)
 
     def scores(qi, kb, seen):
         starts = doc_start(ends, row_positions(z * SPAN + qi * TILE))
@@ -397,11 +397,10 @@
         grad_probs = nt_dot(tile_rows(kv.at[1], kb), grad)
         grad_scores = (probs * (grad_probs - stats[qi, 1:2, :])).astype(bf16)
         if for_key:
-            rows = pl.ds(pl.multiple_of((kb - REACH) * TILE, TILE), TILE)
-            dv_sum[rows, :] += jnp.dot(probs.astype(bf16), grad, preferred_element_type=f32)
-            dk_sum[rows, :] += jnp.dot(grad_scores, query, preferred_element_type=f32)
+            dv_sum[...] += jnp.dot(probs.astype(bf16), grad, preferred_element_type=f32)
+            dk_sum[...] += jnp.dot(grad_scores, query, preferred_element_type=f32)
         if for_query:
-            dq_sum[...] += lax.dot_general(
+            dq_sum[qi] += lax.dot_general(
                 tile_rows(kv.at[0], kb),
                 grad_scores,
                 (((0,), (0,)), ((), ())),
@@ -410,24 +409,24 @@
 
     head_lanes = pl.ds(pl.multiple_of(p * HEAD_DIM, HEAD_DIM), HEAD_DIM)
 
-    def query_back(qi):
-        mine = grads_out.at[0, :, head_lanes]
+    def tile_back(slot, kinds, tile):
+        mine = grads_out.at[kinds, :, head_lanes]
 
         def one(i, carried):
-            r = qi * 8 + lax.rem(i + p, 8)
-            rows = grads.at[0, pl.ds(pl.multiple_of(r * ROWS, ROWS), ROWS), :]
+            r = tile * 8 + lax.rem(i + p, 8)
+            rows = grads.at[kinds, pl.ds(pl.multiple_of(r * ROWS, ROWS), ROWS), :]
 
             @pl.when(r == p)
             def _():
-                pltpu.make_async_copy(rows, mine, recv_sem.at[6]).start()
+                pltpu.make_async_copy(rows, mine, recv_sem.at[slot]).start()
 
             @pl.when(r != p)
             def _():
                 pltpu.make_async_remote_copy(
                     src_ref=rows,
                     dst_ref=mine,
-                    send_sem=send_sem.at[6],
-                    recv_sem=recv_sem.at[6],
+                    send_sem=send_sem.at[slot],
+                    recv_sem=recv_sem.at[slot],
                     device_id=device_of(z, r),
                     device_id_type=MESH,
                 ).start()
@@ -436,52 +435,71 @@
 
         lax.fori_loop(0, 8, one, 0)
 
-    def own_grads(i, carried):
-        qi = lax.rem(i + lax.div(p, 8), NEAR)
-        dq_sum[...] = jnp.zeros_like(dq_sum)
-
-        def probs_of(kb):
-            slot = qi * REACH + kb
-            return saved[slot] * jnp.exp2(tops[slot, 0:1, :] - stats[qi, 0:1, :])
+    def kept_probs(qi, kb):
+        slot = qi * REACH + kb
+        return saved[slot] * jnp.exp2(tops[slot, 0:1, :] - stats[qi, 0:1, :])
+
+    def later_probs(qi, kb):
+        starts = doc_start(ends, row_positions(z * SPAN + qi * TILE))
+        s = nt_dot(tile_rows(kv.at[0], kb), tile_rows(qg.at[0], qi)) * LOG2_SCALE
+        s = s - stats[qi, 0:1, :]
+        return jnp.where(seen_before(z, kb, starts), jnp.exp2(s), 0.0)
+
+    def key_grads(i, carried):
+        tile = lax.rem(i + lax.div(p, 8), NEAR)
+        kb = tile + REACH
+        dk_sum[...] = jnp.zeros_like(dk_sum)
+        dv_sum[...] = jnp.zeros_like(dv_sum)
+
+        def within(qi, inner):
+            add_pair(qi, kb, kept_probs(qi, kb), True, True)
+            return inner
+
+        def after(qi, inner):
+            add_pair(qi, kb, later_probs(qi, kb), False, True)
+            return inner
+
+        lax.fori_loop(tile, NEAR, within, 0)
+        lax.fori_loop(NEAR, kb + 1, after, 0)
+        rows = pl.ds(pl.multiple_of(tile * TILE, TILE), TILE)
+        grads[1, rows, :] = (dk_sum[...] * SCALE).astype(bf16)
+        grads[2, rows, :] = dv_sum[...].astype(bf16)
+        tile_back(7, pl.ds(1, 2), tile)
+        return carried
+
+    def query_grads(i, carried):
+        tile = lax.rem(i + lax.div(p, 8), NEAR)
 
         def before(kb, inner):
-            add_pair(qi, kb, probs_of(kb), True, False)
+            add_pair(tile, kb, kept_probs(tile, kb), True, False)
             return inner
 
-        def within(kb, inner):
-            add_pair(qi, kb, probs_of(kb), True, True)
-            return inner
-
-        lax.fori_loop(qi, REACH, before, 0)
-        lax.fori_loop(REACH, REACH + qi + 1, within, 0)
-        rows = pl.ds(pl.multiple_of(qi * TILE, TILE), TILE)
-        grads[0, rows, :] = (dq_sum[...].T * SCALE).astype(bf16)
-        query_back(qi)
-        return carried
-
-    def later_grads(qi, carried):
-        starts = doc_start(ends, row_positions(z * SPAN + qi * TILE))
-
-        def after(kb, inner):
-            s = nt_dot(tile_rows(kv.at[0], kb), tile_rows(qg.at[0], qi)) * LOG2_SCALE
-            s = s - stats[qi, 0:1, :]
-            probs = jnp.where(seen_before(z, kb, starts), jnp.exp2(s), 0.0)
-            add_pair(qi, kb, probs, False, True)
-            return inner
-
-        lax.fori_loop(jnp.maximum(qi, REACH), REACH + NEAR, after, 0)
-        return carried
-
+        lax.fori_loop(tile, REACH, before, 0)
+        rows = pl.ds(pl.multiple_of(tile * TILE, TILE), TILE)
+        grads[0, rows, :] = (dq_sum[tile].T * SCALE).astype(bf16)
+        tile_back(6, pl.ds(0, 1), tile)
+        return carried
+
+    wait_bytes(kv.at[0, pl.ds(back, SPAN), :], recv_sem.at[0])
+    key_hops(0, 0, 1)
+    wait_bytes(qg.at[0, pl.ds(0, SPAN), :], recv_sem.at[1])
+    query_hops(0, 2, 3)
+    send(2, conv_columns(pair, 0), conv.at[0, :, my_rows(size), :])
     lax.fori_loop(0, NEAR, own_tiles, 0)
+    wait_bytes(kv.at[1, pl.ds(back, SPAN), :], recv_sem.at[9])
+    wait_bytes(qg.at[1, pl.ds(0, SPAN), :], recv_sem.at[10])
+    query_hops(1, 15, 16)
+    send(4, conv_columns(pair, 1), conv.at[1, :, my_rows(size), :])
     wait_bytes(delta, recv_sem.at[3])
+    hops[0].wait()
+    hops[1].wait()
+    key_hops(1, 13, 14)
+    lax.fori_loop(0, NEAR, earlier_tiles, 0)
+    hop(8, stats.at[pl.ds(0, NEAR)], stats.at[pl.ds(NEAR, NEAR)], 3)
+    hop(9, stats.at[pl.ds(0, 1)], stats.at[pl.ds(2 * NEAR, 1)], 2)
     halo(0)
     conv_half(0)
     halo(1)
-    hops[0].wait()
-    hops[1].wait()
-    lax.fori_loop(0, NEAR, earlier_tiles, 0)
-    hop(8, stats.at[pl.ds(0, NEAR)], stats.at[pl.ds(NEAR, NEAR)], 3)
-    hop(9, stats.at[pl.ds(0, 1)], stats.at[pl.ds(2 * NEAR, 1)], 2)
     conv_half(1)
 
     def fold(group, carried):
@@ -497,11 +515,12 @@
     for step in range(1, 8):
         total = total + pltpu.roll(folded[:, step, :], size - step, 1)
     taps[0] = total
-    dk_sum[...] = jnp.zeros_like(dk_sum)
-    dv_sum[...] = jnp.zeros_like(dv_sum)
+    dq_sum[...] = jnp.zeros_like(dq_sum)
     for step in range(1, PLANES):
         hop(9 + step, taps.at[0], taps.at[step], step)
-    lax.fori_loop(0, NEAR, own_grads, 0)
+    for slot in (2, 3, 15, 16, 8, 9):
+        hops[slot].wait()
+    lax.fori_loop(0, NEAR, key_grads, 0)
     for step in range(1, PLANES):
         hops[9 + step].wait()
     tap_total[...] = jnp.dot(
@@ -510,18 +529,9 @@
         precision=lax.Precision.HIGHEST,
         preferred_element_type=f32,
     )
-    hops[8].wait()
-    hops[9].wait()
-    hops[2].wait()
-    hops[3].wait()
-    lax.fori_loop(NEAR, NEAR + REACH, later_grads, 0)
-    grads[1] = (dk_sum[...] * SCALE).astype(bf16)
-    grads[2] = dv_sum[...].astype(bf16)
-    send(
-        7,
-        lambda r: grads.at[pl.ds(1, 2), pl.ds(pl.multiple_of(r * ROWS, ROWS), ROWS), :],
-        grads_out.at[pl.ds(1, 2), :, head_lanes],
-    )
+    hops[13].wait()
+    hops[14].wait()
+    lax.fori_loop(0, NEAR, query_grads, 0)
     tap_rows = taps_out.at[
         pl.ds(pl.multiple_of(lax.div(p, 4) * CONV_GROUPS, CONV_GROUPS), CONV_GROUPS), :
     ]
@@ -540,15 +550,15 @@
 
     lax.fori_loop(1, PLANE // 4, tell, 0)
     most = PLANE - 1
-    wait_bytes(kv.at[:, pl.ds(0, most * ROWS), :], send_sem.at[0])
-    wait_bytes(qg.at[:, pl.ds(0, most * ROWS), :], send_sem.at[1])
+    for slot in (0, 1, 9, 10):
+        wait_bytes(kv.at[0, pl.ds(0, most * ROWS), :], send_sem.at[slot])
     wait_bytes(conv.at[0, :, pl.ds(0, most * ROWS), :], send_sem.at[2])
     wait_bytes(delta.at[pl.ds(0, most)], send_sem.at[3])
     wait_bytes(conv.at[1, :, pl.ds(0, most * ROWS), :], send_sem.at[4])
     wait_bytes(back_out.at[:, :, pl.ds(0, most * CONV_WIDTH)], send_sem.at[5])
     wait_bytes(back_out, recv_sem.at[5])
-    wait_bytes(grads.at[0, pl.ds(0, most * ROWS), :], send_sem.at[6])
-    wait_bytes(grads_out.at[0], recv_sem.at[6])
+    wait_bytes(grads.at[pl.ds(0, 1), pl.ds(0, most * ROWS), :], send_sem.at[6])
+    wait_bytes(grads_out.at[pl.ds(0, 1)], recv_sem.at[6])
     wait_bytes(grads.at[pl.ds(1, 2), pl.ds(0, most * ROWS), :], send_sem.at[7])
     wait_bytes(grads_out.at[pl.ds(1, 2)], recv_sem.at[7])
     wait_bytes(taps_out.at[pl.ds(0, FILTER_LEN - CONV_GROUPS), :], send_sem.at[8])
@@ -594,12 +604,12 @@
             vmem((NEAR, 8, TILE), f32),
             vmem((NEAR * (REACH + 1), TILE, TILE), f32),
             vmem((NEAR * (REACH + 1), 8, TILE), f32),
-            vmem((SPAN, HEAD_DIM), f32),
-            vmem((SPAN, HEAD_DIM), f32),
-            vmem((HEAD_DIM, TILE), f32),
+            vmem((TILE, HEAD_DIM), f32),
+            vmem((TILE, HEAD_DIM), f32),
+            vmem((NEAR, HEAD_DIM, TILE), f32),
             vmem((3, SPAN, HEAD_DIM), bf16),
             vmem((CONV_GROUPS, FILTER_LEN), f32),
-            dma((9,)), dma((9,)), dma((9,)), dma((13,)), dma((13,)),
+            dma((9,)), dma((11,)), dma((11,)), dma((17,)), dma((17,)),
         ],
         compiler_params=pltpu.CompilerParams(
             collective_id=0, has_side_effects=True, vmem_limit_bytes=VMEM_LIMIT

time: 84 us -> 74.2 us (0.88)
  Pallas kernels: 82.1 us -> 72.8 us
    pallas_call x1, Pallas kernels: 77.9 us -> 68.7 us  [exchange(): pl.pallas_call(exchange_kernel, out_shape=(shape((3, ROWS, features), bf1...]
where the time goes in v4:
time: 74.2 us; the launch traced here: 73.5 us
  Pallas kernels  72.8 us (98%)
    pallas_call x1, Pallas kernels, exchange(): pl.pallas_call(exchange_kernel, out_shape=(shape((3, ROWS, features), bf1...  68.7 us
    pallas_call x1, Pallas kernels, finish(): pl.pallas_call(finish_kernel, grid=(FINISH_STEPS,), out_shape=(attn,) * 3...  4.14 us

profile of v4, /device:TPU:0, one launch (start us, length us, event | category | flops | bytes accessed | tf_op | source)
XLA Modules:
  0.0 73.5 jit_solution(311178312724392895)
XLA Ops:
  0.6 68.7 %exchange.1 = (bf16[3,32,4096]{2,1,0:T(8,128)(2,1)}, bf16[2,32,8192]{2,1,0:T(8,128)(2,1)}, f32[128,128]{1,0:T(8,128)}) custom-call(s32[12]{0:T(128)} %len_ref.1, bf16[32,4096]{1,0:T(8,128)(2,1)} %q.1, bf16[32,4096]{1,0:T(8,128)(2,1)} %k.1, bf16[32,4096]{1,0:T(8,128)(2,1)} %v.1, bf16[32,4096]{1,0:T(8,128)(2,1)} %o.1, bf16[32,4096]{1,0:T(8,128)(2,1)} %g.1, ...), custom_call_target="tpu_custom_call" | custom-call | tf_op jit(solution)/shard_map/exchange/pallas_call | solution.py:575
  69.3 4.1 %finish.1 = (bf16[32,4096]{1,0:T(8,128)(2,1)}, bf16[32,4096]{1,0:T(8,128)(2,1)}, bf16[32,4096]{1,0:T(8,128)(2,1)}, bf16[32,8192]{1,0:T(8,128)(2,1)}, bf16[32,819...) custom-call(bf16[3,32,4096]{2,1,0:T(8,128)(2,1)} %get-tuple-element.10.grads, ...), custom_call_target="tpu_custom_call" | custom-call | tf_op jit(solution)/shard_map/finish/pallas_call | solution.py:648

commit v5 on v4

--- a/solution.py
+++ b/solution.py
@@ -630,7 +630,7 @@
     gcv[...] = (inner * ck[...].astype(f32)).astype(bf16)
 
 
-FINISH_STEPS = 4
+FINISH_STEPS = 2
 
 
 def finish(grads, taps, back, cg, cv, ck):

time: 74.2 us -> 73.1 us (0.985)
  Pallas kernels: 72.8 us -> 71.8 us
    pallas_call x1, Pallas kernels: 4.14 us -> 3.08 us  [finish(): pl.pallas_call(finish_kernel, grid=(FINISH_STEPS,), out_shape=(attn,) * 3...]
where the time goes in v5:
time: 73.1 us; the launch traced here: 72.4 us
  Pallas kernels  71.8 us (98%)
    pallas_call x1, Pallas kernels, exchange(): pl.pallas_call(exchange_kernel, out_shape=(shape((3, ROWS, features), bf1...  68.7 us
    pallas_call x1, Pallas kernels, finish(): pl.pallas_call(finish_kernel, grid=(FINISH_STEPS,), out_shape=(attn,) * 3...  3.08 us

profile of v5, /device:TPU:0, one launch (start us, length us, event | category | flops | bytes accessed | tf_op | source)
XLA Modules:
  0.0 72.4 jit_solution(7026623148846863811)
XLA Ops:
  0.6 68.7 %exchange.1 = (bf16[3,32,4096]{2,1,0:T(8,128)(2,1)}, bf16[2,32,8192]{2,1,0:T(8,128)(2,1)}, f32[128,128]{1,0:T(8,128)}) custom-call(s32[12]{0:T(128)} %len_ref.1, bf16[32,4096]{1,0:T(8,128)(2,1)} %q.1, bf16[32,4096]{1,0:T(8,128)(2,1)} %k.1, bf16[32,4096]{1,0:T(8,128)(2,1)} %v.1, bf16[32,4096]{1,0:T(8,128)(2,1)} %o.1, bf16[32,4096]{1,0:T(8,128)(2,1)} %g.1, ...), custom_call_target="tpu_custom_call" | custom-call | tf_op jit(solution)/shard_map/exchange/pallas_call | solution.py:575
  69.3 3.1 %finish.1 = (bf16[32,4096]{1,0:T(8,128)(2,1)}, bf16[32,4096]{1,0:T(8,128)(2,1)}, bf16[32,4096]{1,0:T(8,128)(2,1)}, bf16[32,8192]{1,0:T(8,128)(2,1)}, bf16[32,819...) custom-call(bf16[3,32,4096]{2,1,0:T(8,128)(2,1)} %get-tuple-element.10.grads, ...), custom_call_target="tpu_custom_call" | custom-call | tf_op jit(solution)/shard_map/finish/pallas_call | solution.py:648

commit v6 on v5

--- a/solution.py
+++ b/solution.py
@@ -121,7 +121,7 @@
     len_ref, q, k, v, o, g, cq, ck, cv, cg, filt,
     grads_out, back_out, taps_out,
     kv_in, qg_in, o_in, conv_in, pair, delta_in, delta, kv, qg, conv, result, circ, back_circ,
-    tap_sum, folded, taps, stats, running, saved, tops, dk_sum, dv_sum, dq_sum, grads, tap_total,
+    tap_sum, folded, taps, stats, running, saved, tops, dk_sum, dv_sum, dq_sum, grads, tap_total, masks, seen_taps,
     load_sem, send_sem, recv_sem, zsend_sem, zrecv_sem,
 ):
     z, p = place_in_slice()
@@ -295,20 +295,28 @@
     group_of_lane = lax.div(across, 16)
 
     def conv_tile(half, tb):
-        base = z * SPAN + tb * size
-        positions = base + lax.broadcasted_iota(jnp.int32, (1, size), 1)
-
-        def as_column(row):
-            return jnp.broadcast_to(row.astype(f32), (size, size)).T.astype(jnp.int32)
-
-        start = as_column(doc_start(ends, positions))
-        stop = as_column(doc_stop(ends, positions))
-        prev = jnp.where((across > down) & (base - size + across >= start), 1.0, 0.0)
-        here = jnp.where((across <= down) & (base + across >= start), 1.0, 0.0)
-        ahead = jnp.where((across >= down) & (base + across < stop), 1.0, 0.0)
-        beyond = jnp.where((across < down) & (base + size + across < stop), 1.0, 0.0)
-        prev_b, here_b = prev.astype(bf16), here.astype(bf16)
-        ahead_b, beyond_b = ahead.astype(bf16), beyond.astype(bf16)
+        if half == 0:
+            base = z * SPAN + tb * size
+            positions = base + lax.broadcasted_iota(jnp.int32, (1, size), 1)
+
+            def as_column(row):
+                return jnp.broadcast_to(row.astype(f32), (size, size)).T.astype(jnp.int32)
+
+            start = as_column(doc_start(ends, positions))
+            stop = as_column(doc_stop(ends, positions))
+            prev = jnp.where((across > down) & (base - size + across >= start), 1.0, 0.0)
+            here = jnp.where((across <= down) & (base + across >= start), 1.0, 0.0)
+            ahead = jnp.where((across >= down) & (base + across < stop), 1.0, 0.0)
+            beyond = jnp.where((across < down) & (base + size + across < stop), 1.0, 0.0)
+            prev_b, here_b = prev.astype(bf16), here.astype(bf16)
+            ahead_b, beyond_b = ahead.astype(bf16), beyond.astype(bf16)
+            for kind, mask in enumerate((prev_b, here_b, ahead_b, beyond_b)):
+                masks[tb, kind] = mask
+            seen = prev + here
+            seen_taps[tb] = seen
+        else:
+            prev_b, here_b, ahead_b, beyond_b = (masks[tb, kind] for kind in range(4))
+            seen = seen_taps[tb]
         rows = pl.ds(pl.multiple_of(tb * size, size), size)
         here_rows = pl.ds(pl.multiple_of(tb * size + size, size), size)
         mixed = conv[half, 0, pl.ds(pl.multiple_of(tb * size, size), 2 * size), :]
@@ -340,7 +348,7 @@
                 inner,
             )
             outer = nt_dot(jnp.where(chosen, own, jnp.zeros_like(own)), mixed)
-            tap_sum[group] += outer[:, :size] * prev + outer[:, size:] * here
+            tap_sum[group] += jnp.where(across > down, outer[:, :size], outer[:, size:]) * seen
         result[half, 0, rows, :] = out.astype(bf16)
         result[half, 1, rows, :] = inner.astype(bf16)
 
@@ -609,6 +617,8 @@
             vmem((NEAR, HEAD_DIM, TILE), f32),
             vmem((3, SPAN, HEAD_DIM), bf16),
             vmem((CONV_GROUPS, FILTER_LEN), f32),
+            vmem((SPAN // FILTER_LEN, 4, FILTER_LEN, FILTER_LEN), bf16),
+            vmem((SPAN // FILTER_LEN, FILTER_LEN, FILTER_LEN), f32),
             dma((9,)), dma((11,)), dma((11,)), dma((17,)), dma((17,)),
         ],
         compiler_params=pltpu.CompilerParams(

time: 73.1 us -> 72.4 us (level)
  no operation moved by 1% of the time
where the time goes in v6:
time: 72.4 us; the launch traced here: 71.7 us
  Pallas kernels  71.1 us (98%)
    pallas_call x1, Pallas kernels, exchange(): pl.pallas_call(exchange_kernel, out_shape=(shape((3, ROWS, features), bf1...  68 us
    pallas_call x1, Pallas kernels, finish(): pl.pallas_call(finish_kernel, grid=(FINISH_STEPS,), out_shape=(attn,) * 3...  3.08 us

profile of v6, /device:TPU:0, one launch (start us, length us, event | category | flops | bytes accessed | tf_op | source)
XLA Modules:
  0.0 71.7 jit_solution(14670052089174674234)
XLA Ops:
  0.6 68.0 %exchange.1 = (bf16[3,32,4096]{2,1,0:T(8,128)(2,1)}, bf16[2,32,8192]{2,1,0:T(8,128)(2,1)}, f32[128,128]{1,0:T(8,128)}) custom-call(s32[12]{0:T(128)} %len_ref.1, bf16[32,4096]{1,0:T(8,128)(2,1)} %q.1, bf16[32,4096]{1,0:T(8,128)(2,1)} %k.1, bf16[32,4096]{1,0:T(8,128)(2,1)} %v.1, bf16[32,4096]{1,0:T(8,128)(2,1)} %o.1, bf16[32,4096]{1,0:T(8,128)(2,1)} %g.1, ...), custom_call_target="tpu_custom_call" | custom-call | tf_op jit(solution)/shard_map/exchange/pallas_call | solution.py:583
  68.7 3.1 %finish.1 = (bf16[32,4096]{1,0:T(8,128)(2,1)}, bf16[32,4096]{1,0:T(8,128)(2,1)}, bf16[32,4096]{1,0:T(8,128)(2,1)}, bf16[32,8192]{1,0:T(8,128)(2,1)}, bf16[32,819...) custom-call(bf16[3,32,4096]{2,1,0:T(8,128)(2,1)} %get-tuple-element.10.grads, ...), custom_call_target="tpu_custom_call" | custom-call | tf_op jit(solution)/shard_map/finish/pallas_call | solution.py:658
